TPU v7x, 256 devices: a whole 4x4x8 slice. The times are simulated.
256 devices in a mesh: dp: 16 (over y, z_hi), tensor: 16 (over z_lo, x, core).
Axes of the slice: x: 4, y: 4, z: 8 (z_hi: 4, z_lo: 2; z = z_hi * 2 + z_lo), core: 2. Of those that a mesh axis runs over, the one named last changes fastest.
Arguments:
- tokens: bfloat16 [768, 8192], P('tensor', 'dp'), may hold values from -6 to 6
- w_gate: bfloat16 [8192, 28672], P('dp', 'tensor'), may hold values from -0.0625 to 0.0625
- w_up: bfloat16 [8192, 28672], P('dp', 'tensor'), may hold values from -0.0625 to 0.0625
- w_down: bfloat16 [28672, 8192], P('tensor', 'dp'), may hold values from -0.03125 to 0.03125
- cotangent: bfloat16 [768, 8192], P('tensor', 'dp'), may hold values from -6 to 6
Outputs:
- d_tokens: bfloat16 [768, 8192], P('tensor', 'dp')
- d_gate: bfloat16 [8192, 28672], P('dp', 'tensor')
- d_up: bfloat16 [8192, 28672], P('dp', 'tensor')
- d_down: bfloat16 [28672, 8192], P('tensor', 'dp')
All inputs are finite; a program needn't handle non-finite values.
Results may differ from a plain program's by a relative error of at most 0.0057.
Values may be sent and summed in bfloat16 or wider, within the bound.
A program may use at most 128 MiB of HBM per device.

v0:
```python
import math

import jax
import jax.numpy as jnp
from jax import lax
from jax.sharding import PartitionSpec as P

BLK = 128


def swapped(value, axis, distance):
    mask = 2**distance
    pairs = [(source, source ^ mask) for source in range(lax.axis_size(axis))]
    return lax.ppermute(value, axis, pairs)


def sylvester(order):
    positions = jnp.arange(order, dtype=jnp.int32)
    row_ids = positions[:, None]
    col_ids = positions[None, :]
    signs = jnp.ones((order, order), jnp.float32)
    for power in range(order.bit_length() - 1):
        both = (row_ids >> power & 1) * (col_ids >> power & 1)
        signs = signs * (1 - 2 * both).astype(jnp.float32)
    return signs


def rotate(values):
    row_count, width = values.shape
    shaped = values.reshape(row_count, width // BLK, BLK)
    inner = jnp.einsum("mbj,jk->mbk", shaped, sylvester(BLK), precision=lax.Precision.HIGHEST)
    inner = inner.reshape(row_count, width)
    members = lax.axis_size("tensor")
    position = lax.axis_index("tensor")
    mixed = inner
    for power in range(members.bit_length() - 1):
        partner = swapped(mixed, "tensor", power)
        upper = position >> power & 1 == 1
        mixed = jnp.where(upper, partner - mixed, mixed + partner)
    return mixed * (1.0 / math.sqrt(BLK * members))


def per_device(tokens, w_gate, w_up, w_down, cotangent):
    all_tokens, all_cotangent = (
        lax.all_gather(tokens, "tensor", axis=0, tiled=True),
        lax.all_gather(cotangent, "tensor", axis=0, tiled=True),
    )
    width = w_gate.shape[1]
    paired = jnp.concatenate((w_gate, w_up), axis=1)
    block_rows = all_tokens
    sums = lax.psum_scatter(
        jnp.dot(block_rows, paired, preferred_element_type=jnp.float32),
        "dp",
        scatter_dimension=0,
        tiled=True,
    )
    gate = sums[:, :width]
    up = sums[:, width:]
    sigma = jax.nn.sigmoid(gate)
    silu_gate = gate * sigma
    hidden = (silu_gate * up).astype(jnp.bfloat16)
    rotated = rotate(hidden.astype(jnp.float32)).astype(jnp.bfloat16)
    block_rows = all_cotangent
    d_down = lax.dot_general(
        lax.all_gather(rotated, "dp", axis=0, tiled=True),
        block_rows,
        (((0,), (0,)), ((), ())),
        preferred_element_type=jnp.float32,
    ).astype(jnp.bfloat16)
    block_rows = all_cotangent
    d_rotated = lax.psum_scatter(
        lax.dot_general(
            block_rows, w_down, (((1,), (1,)), ((), ())), preferred_element_type=jnp.float32
        ),
        "dp",
        scatter_dimension=0,
        tiled=True,
    )
    d_hidden = rotate(d_rotated)
    d_gate_pre = (d_hidden * up * sigma * (1.0 + gate * (1.0 - sigma))).astype(jnp.bfloat16)
    d_up_pre = (d_hidden * silu_gate).astype(jnp.bfloat16)
    grads_gate, grads_up = (
        lax.all_gather(d_gate_pre, "dp", axis=0, tiled=True),
        lax.all_gather(d_up_pre, "dp", axis=0, tiled=True),
    )
    contract_rows = (((0,), (0,)), ((), ()))
    d_gate = lax.dot_general(
        all_tokens, grads_gate, contract_rows, preferred_element_type=jnp.float32
    ).astype(jnp.bfloat16)
    d_up = lax.dot_general(
        all_tokens, grads_up, contract_rows, preferred_element_type=jnp.float32
    ).astype(jnp.bfloat16)
    contract_cols = (((1,), (1,)), ((), ()))
    first = lax.dot_general(grads_gate, w_gate, contract_cols, preferred_element_type=jnp.float32)
    second = lax.dot_general(grads_up, w_up, contract_cols, preferred_element_type=jnp.float32)
    d_tokens = lax.psum_scatter(first + second, "tensor", scatter_dimension=0, tiled=True).astype(
        jnp.bfloat16
    )
    return (d_tokens, d_gate, d_up, d_down)


def solution(mesh):
    return jax.shard_map(
        per_device,
        mesh=mesh,
        in_specs=(
            P("tensor", "dp"),
            P("dp", "tensor"),
            P("dp", "tensor"),
            P("tensor", "dp"),
            P("tensor", "dp"),
        ),
        out_specs=(P("tensor", "dp"), P("dp", "tensor"), P("dp", "tensor"), P("tensor", "dp")),
        check_vma=False,
    )
```

profile of v0, /device:TPU:8, one launch (start us, length us, event | category | flops | bytes accessed | tf_op | source)
XLA Modules:
  0.0 563.7 jit_solution(6861895912413155297)
XLA Ops:
  7.2 22.6 %all_gather.15 = bf16[768,512]{1,0:T(8,128)(2,1)S(1)} all-gather(bf16[48,512]{1,0:T(8,128)(2,1)} %param.9), channel_id=1, replica_groups=mesh['dp'=16,'tensor'=16] {'tensor'}, dimensions={0}, use_global_device_ids=true | all-gather | bytes 835584 | tf_op jit(solution)/shard_map/all_gather | solution.py:46
  29.8 4.1 fusion.18
  34.7 21.8 %all_gather.16 = bf16[768,512]{1,0:T(8,128)(2,1)} all-gather(bf16[48,512]{1,0:T(8,128)(2,1)S(1)} %copy-done.1), channel_id=1, replica_groups=mesh['dp'=16,'tensor'=16] {'tensor'}, dimensions={0}, use_global_device_ids=true | all-gather | bytes 835584 | tf_op jit(solution)/shard_map/all_gather | solution.py:45
  56.5 9.4 %convolution_bitcast_fusion = f32[768,3584]{0,1:T(8,128)} fusion(bf16[768,512]{1,0:T(8,128)(2,1)} %all_gather.16, bf16[512,1792]{1,0:T(8,128)(2,1)} %param.7, bf16[512,1792]{1,0:T(8,128)(2,1)} %param.6), kind=kOutput, calls=%fused_computation | convolution fusion | flops 2825912320 | bytes 15466496 | tf_op jit(solution)/shard_map/dot_general | solution.py:52
  65.9 12.2 %copy.38 = f32[768,3584]{1,0:T(8,128)} copy(f32[768,3584]{0,1:T(8,128)} %convolution_bitcast_fusion) | data formatting | bytes 22020096
  78.2 59.4 %reduce-scatter.6.cloned.1.call-done = f32[48,1792]{1,0:T(8,128)} async-done(((f32[768,1792]{1,0:T(8,128)}), f32[48,1792]{1,0:T(8,128)}) %reduce-scatter.6.cloned.1.call-update) | async-done | bytes 344080 | tf_op jit(solution)/shard_map/reduce_scatter | solution.py:71
  143.7 8.8 %collective-permute-done.1 = f32[48,1792]{1,0:T(8,128)} collective-permute-done((f32[48,1792]{1,0:T(8,128)S(1)}, f32[48,1792]{1,0:T(8,128)}, u32[]{:S(2)}, u32[]{:S(2)}) %collective-permute-start.1) | collective-permute-done | bytes 344096 | tf_op jit(solution)/shard_map/ppermute | solution.py:14
  156.5 7.9 %collective-permute-done.2 = f32[48,1792]{1,0:T(8,128)} collective-permute-done((f32[48,1792]{1,0:T(8,128)S(1)}, f32[48,1792]{1,0:T(8,128)}, u32[]{:S(2)}, u32[]{:S(2)}) %collective-permute-start.2) | collective-permute-done | bytes 344096 | tf_op jit(solution)/shard_map/ppermute | solution.py:14
  166.8 24.6 %collective-permute-done.3 = f32[48,1792]{1,0:T(8,128)S(1)} collective-permute-done((f32[48,1792]{1,0:T(8,128)S(1)}, f32[48,1792]{1,0:T(8,128)S(1)}, u32[]{:S(2)}, u32[]{:S(2)}) %collective-permute-start.3) | collective-permute-done | bytes 344096 | tf_op jit(solution)/shard_map/ppermute | solution.py:14
  191.4 101.2 %reduce-scatter.10.cloned.1.call-done = f32[48,3584]{1,0:T(8,128)} async-done(((f32[768,3584]{1,0:T(8,128)}), f32[48,3584]{1,0:T(8,128)}) %reduce-scatter.10.cloned.1.call-update) | async-done | bytes 688144 | tf_op jit(solution)/shard_map/reduce_scatter | solution.py:51
  299.1 8.6 %collective-permute-done.5 = f32[48,1792]{1,0:T(8,128)S(1)} collective-permute-done((f32[48,1792]{1,0:T(8,128)S(1)}, f32[48,1792]{1,0:T(8,128)S(1)}, u32[]{:S(2)}, u32[]{:S(2)}) %collective-permute-start.5) | collective-permute-done | bytes 344096 | tf_op jit(solution)/shard_map/ppermute | solution.py:14
  310.8 7.8 %collective-permute-done.6 = f32[48,1792]{1,0:T(8,128)S(1)} collective-permute-done((f32[48,1792]{1,0:T(8,128)S(1)}, f32[48,1792]{1,0:T(8,128)S(1)}, u32[]{:S(2)}, u32[]{:S(2)}) %collective-permute-start.6) | collective-permute-done | bytes 344096 | tf_op jit(solution)/shard_map/ppermute | solution.py:14
  318.8 9.5 %collective-permute-done.7 = f32[48,1792]{1,0:T(8,128)S(1)} collective-permute-done((f32[48,1792]{1,0:T(8,128)S(1)}, f32[48,1792]{1,0:T(8,128)S(1)}, u32[]{:S(2)}, u32[]{:S(2)}) %collective-permute-start.7) | collective-permute-done | bytes 344096 | tf_op jit(solution)/shard_map/ppermute | solution.py:14
  329.2 29.8 %all-gather.4.cloned.1.call-done = bf16[768,1792]{1,0:T(8,128)(2,1)} async-done(((bf16[48,1792]{1,0:T(8,128)(2,1)}), bf16[768,1792]{1,0:T(8,128)(2,1)}) %all-gather.4.cloned.1.call-update) | async-done | bytes 2752528 | tf_op jit(solution)/shard_map/all_gather | solution.py:83
  359.0 5.1 fusion.19
  364.1 60.6 %all-gather.6.cloned.1.call-done = bf16[768,1792]{1,0:T(8,128)(2,1)} async-done(((bf16[48,1792]{1,0:T(8,128)(2,1)}), bf16[768,1792]{1,0:T(8,128)(2,1)}) %all-gather.6.cloned.1.call-update) | async-done | bytes 2752528 | tf_op jit(solution)/shard_map/all_gather | solution.py:84
  424.7 5.6 convolution_add_fusion
  430.3 4.8 fusion.3
  435.1 3.8 copy.36
  438.9 4.8 fusion.4
  443.8 3.8 copy.37
  447.6 42.2 %all-gather.8.cloned.1.call-done = bf16[768,1792]{1,0:T(8,128)(2,1)} async-done(((bf16[48,1792]{1,0:T(8,128)(2,1)}), bf16[768,1792]{1,0:T(8,128)(2,1)}) %all-gather.8.cloned.1.call-update) | async-done | bytes 2752528 | tf_op jit(solution)/shard_map/all_gather | solution.py:65
  489.7 4.6 convolution_convert_fusion
  494.4 60.9 %reduce-scatter.8.cloned.1.call-done = f32[48,512]{1,0:T(8,128)} async-done(((f32[768,512]{1,0:T(8,128)}), f32[48,512]{1,0:T(8,128)}) %reduce-scatter.8.cloned.1.call-update) | async-done | bytes 98320 | tf_op jit(solution)/shard_map/reduce_scatter | solution.py:96
  (43 shorter events, 25.6 us)
Async XLA Ops:
  7.2 22.6 %copy-start = (bf16[1792,512]{1,0:T(8,128)(2,1)S(1)}, bf16[1792,512]{1,0:T(8,128)(2,1)}, u32[]{:S(2)}) copy-start(bf16[1792,512]{1,0:T(8,128)(2,1)} %param.8) | copy-start | bytes 5505028
  7.2 130.4 %reduce-scatter.6.cloned.1.call-start = ((), (), s32[]{:S(2)}) async-start(), calls=%async_computation.3 | async-start | bytes 5849088 | tf_op jit(solution)/shard_map/reduce_scatter | solution.py:71
  33.9 0.8 copy-start.1
  33.9 258.7 %reduce-scatter.10.cloned.1.call-start = ((), (), s32[]{:S(2)}) async-start(), calls=%async_computation.8 | async-start | bytes 11698176 | tf_op jit(solution)/shard_map/reduce_scatter | solution.py:51
  78.1 280.9 %all-gather.4.cloned.1.call-start = ((), (), s32[]{:S(2)}) async-start(), calls=%async_computation.4 | async-start | bytes 2924544 | tf_op jit(solution)/shard_map/all_gather | solution.py:83
  139.2 1.9 collective-permute-start
  142.1 10.3 %collective-permute-start.1 = (f32[48,1792]{1,0:T(8,128)S(1)}, f32[48,1792]{1,0:T(8,128)}, u32[]{:S(2)}, u32[]{:S(2)}) collective-permute-start(f32[48,1792]{1,0:T(8,128)S(1)} %add_select_fusion.5), channel_id=1, source_target_pairs={{0,2},{1,3},{2,0},{3,1},{4,6},{5,7},{6,4},{7,5},{8,10},{9,11},{10,... | collective-permute-start | bytes 1032200 | tf_op jit(solution)/shard_map/ppermute | solution.py:14
  153.5 11.0 %collective-permute-start.2 = (f32[48,1792]{1,0:T(8,128)S(1)}, f32[48,1792]{1,0:T(8,128)}, u32[]{:S(2)}, u32[]{:S(2)}) collective-permute-start(f32[48,1792]{1,0:T(8,128)S(1)} %add_select_fusion.4), channel_id=1, source_target_pairs={{0,4},{1,5},{2,6},{3,7},{4,0},{5,1},{6,2},{7,3},{8,12},{9,13},{10,... | collective-permute-start | bytes 1032200 | tf_op jit(solution)/shard_map/ppermute | solution.py:14
  165.5 25.9 %collective-permute-start.3 = (f32[48,1792]{1,0:T(8,128)S(1)}, f32[48,1792]{1,0:T(8,128)S(1)}, u32[]{:S(2)}, u32[]{:S(2)}) collective-permute-start(f32[48,1792]{1,0:T(8,128)S(1)} %add_select_fusion.3), channel_id=1, source_target_pairs={{0,8},{1,9},{2,10},{3,11},{4,12},{5,13},{6,14},{7,15},{8,0},{9,1},... | collective-permute-start | bytes 1032200 | tf_op jit(solution)/shard_map/ppermute | solution.py:14
  294.6 130.0 %all-gather.6.cloned.1.call-start = ((), (), s32[]{:S(2)}) async-start(), calls=%async_computation.5 | async-start | bytes 2924544 | tf_op jit(solution)/shard_map/all_gather | solution.py:84
  295.2 194.5 %all-gather.8.cloned.1.call-start = ((), (), s32[]{:S(2)}) async-start(), calls=%async_computation.7 | async-start | bytes 2924544 | tf_op jit(solution)/shard_map/all_gather | solution.py:65
  295.8 1.7 collective-permute-start.4
  297.6 10.2 %collective-permute-start.5 = (f32[48,1792]{1,0:T(8,128)S(1)}, f32[48,1792]{1,0:T(8,128)S(1)}, u32[]{:S(2)}, u32[]{:S(2)}) collective-permute-start(f32[48,1792]{1,0:T(8,128)S(1)} %add_select_fusion.2), channel_id=1, source_target_pairs={{0,2},{1,3},{2,0},{3,1},{4,6},{5,7},{6,4},{7,5},{8,10},{9,11},{10,... | collective-permute-start | bytes 1032200 | tf_op jit(solution)/shard_map/ppermute | solution.py:14
  307.8 10.9 %collective-permute-start.6 = (f32[48,1792]{1,0:T(8,128)S(1)}, f32[48,1792]{1,0:T(8,128)S(1)}, u32[]{:S(2)}, u32[]{:S(2)}) collective-permute-start(f32[48,1792]{1,0:T(8,128)S(1)} %add_select_fusion.1), channel_id=1, source_target_pairs={{0,4},{1,5},{2,6},{3,7},{4,0},{5,1},{6,2},{7,3},{8,12},{9,13},{10,... | collective-permute-start | bytes 1032200 | tf_op jit(solution)/shard_map/ppermute | solution.py:14
  318.7 9.6 %collective-permute-start.7 = (f32[48,1792]{1,0:T(8,128)S(1)}, f32[48,1792]{1,0:T(8,128)S(1)}, u32[]{:S(2)}, u32[]{:S(2)}) collective-permute-start(f32[48,1792]{1,0:T(8,128)S(1)} %add_select_fusion), channel_id=1, source_target_pairs={{0,8},{1,9},{2,10},{3,11},{4,12},{5,13},{6,14},{7,15},{8,0},{9,1},... | collective-permute-start | bytes 1032200 | tf_op jit(solution)/shard_map/ppermute | solution.py:14
  329.0 226.3 %reduce-scatter.8.cloned.1.call-start = ((), (), s32[]{:S(2)}) async-start(), calls=%async_computation.6 | async-start | bytes 1671168 | tf_op jit(solution)/shard_map/reduce_scatter | solution.py:96
Sparse Core Ops, SparseCore 0:
  34.0 103.5 reduce-scatter.5
  141.3 151.1 reduce-scatter.9
  296.0 63.0 all-gather.3
  362.2 62.3 all-gather.5
  427.3 62.3 all-gather.7
  492.3 62.9 reduce-scatter.7
where the time goes:
time: 564 us
  waiting for transfers between devices  425 us (75%)
  blocking collectives  44.4 us (8%)
  matrix products  40.5 us (7%)
  local copies, waits for them, and re-layouts  20.6 us (4%)
  between operations  14.2 us (3%)
  starting transfers between devices  11.3 us (2%)
  other arithmetic  7.49 us (1%)
    reduce_scatter x1, waiting for transfers between devices, per_device(): lax.psum_scatter(jnp.dot(block_rows, paired, preferred_element_type=jnp.f...  101 us
    ppermute x8, waiting for transfers between devices, swapped(): return lax.ppermute(value, axis, pairs)  70.5 us
    reduce_scatter x1, waiting for transfers between devices, per_device(): lax.psum_scatter(first + second, 'tensor', scatter_dimension=0, tiled=True)  60.9 us
    all_gather x1, waiting for transfers between devices, per_device(): lax.all_gather(d_up_pre, 'dp', axis=0, tiled=True)  60.6 us
    reduce_scatter x1, waiting for transfers between devices, per_device(): lax.psum_scatter(lax.dot_general(block_rows, w_down, (((1,), (1,)), ((),...  59.4 us
    all_gather x1, waiting for transfers between devices, per_device(): lax.all_gather(rotated, 'dp', axis=0, tiled=True)  42.2 us
    all_gather x1, waiting for transfers between devices, per_device(): lax.all_gather(d_gate_pre, 'dp', axis=0, tiled=True)  29.8 us
    all_gather x1, blocking collectives, per_device(): lax.all_gather(cotangent, 'tensor', axis=0, tiled=True)  22.6 us
  transfers between devices with their start and end apart: 14, of which 14 were waited for; matrix products, arithmetic and copies ran while one was open for 11% of the time, Pallas kernels for 0%

commit v1 on v0

--- a/solution.py
+++ b/solution.py
@@ -1,11 +1,21 @@
+import functools
 import math
 
 import jax
 import jax.numpy as jnp
 from jax import lax
+from jax.experimental import pallas as pl
+from jax.experimental.pallas import tpu as pltpu
 from jax.sharding import PartitionSpec as P
 
 BLK = 128
+BF = jnp.bfloat16
+F32 = jnp.float32
+MESH = pl.DeviceIdType.MESH
+NQ = 7
+NP = 3 * NQ
+LAG_B, LAG_C, LAG_D, LAG_E = 1, 3, 4, 5
+ROT_0 = NQ + LAG_E
 
 
 def swapped(value, axis, distance):
@@ -14,7 +24,7 @@
     return lax.ppermute(value, axis, pairs)
 
 
-def sylvester(order):
+def sylvester(order, dtype=jnp.float32):
     positions = jnp.arange(order, dtype=jnp.int32)
     row_ids = positions[:, None]
     col_ids = positions[None, :]
@@ -22,7 +32,7 @@
     for power in range(order.bit_length() - 1):
         both = (row_ids >> power & 1) * (col_ids >> power & 1)
         signs = signs * (1 - 2 * both).astype(jnp.float32)
-    return signs
+    return signs.astype(dtype)
 
 
 def rotate(values):
@@ -40,22 +50,335 @@
     return mixed * (1.0 / math.sqrt(BLK * members))
 
 
+class Place:
+    def __init__(self):
+        self.dp = lax.axis_index("dp")
+        self.t = lax.axis_index("tensor")
+        self.y, self.zh = lax.div(self.dp, 4), lax.rem(self.dp, 4)
+        self.zl = lax.div(self.t, 8)
+        self.x = lax.rem(lax.div(self.t, 2), 4)
+        self.core = lax.rem(self.t, 2)
+
+    def at_y(self, step):
+        return lax.rem(self.y + step + 4, 4)
+
+    def at_z(self, step):
+        return lax.rem(self.zh + step + 4, 4)
+
+    def at_x(self, step):
+        return lax.rem(self.x + step + 4, 4)
+
+    def dp_y(self, step):
+        return {"dp": self.at_y(step) * 4 + self.zh, "tensor": self.t}
+
+    def dp_z(self, step):
+        return {"dp": self.y * 4 + self.at_z(step), "tensor": self.t}
+
+    def slot(self, zl, x, core):
+        return zl * 8 + x * 2 + core
+
+    def to_x(self, step):
+        return {"dp": self.dp, "tensor": self.slot(self.zl, self.at_x(step), self.core)}
+
+    def to_core(self):
+        return {"dp": self.dp, "tensor": self.slot(self.zl, self.x, 1 - self.core)}
+
+    def to_zl(self):
+        return {"dp": self.dp, "tensor": self.slot(1 - self.zl, self.x, self.core)}
+
+    def meet(self):
+        peers = [self.dp_y(1), self.dp_y(-1), self.dp_z(1), self.dp_z(-1)]
+        peers += [self.to_x(k) for k in (1, 2, 3)] + [self.to_core(), self.to_zl()]
+        barrier = pltpu.get_barrier_semaphore()
+        for peer in peers:
+            pl.semaphore_signal(barrier, inc=1, device_id=peer, device_id_type=MESH)
+        pl.semaphore_wait(barrier, len(peers))
+
+
+def send(src, dst, send_sem, recv_sem, to):
+    return pltpu.make_async_remote_copy(
+        src_ref=src, dst_ref=dst, send_sem=send_sem, recv_sem=recv_sem, device_id=to, device_id_type=MESH
+    )
+
+
+def sign_of(bit):
+    return (1 - 2 * bit).astype(F32)
+
+
+def x_sign(place, other):
+    both = lax.rem(place.x, 2) * lax.rem(other, 2) + lax.div(place.x, 2) * lax.div(other, 2)
+    return sign_of(lax.rem(both, 2))
+
+
+def inner_hadamard(value, had):
+    parts = []
+    for start in range(0, value.shape[1], BLK):
+        block = value[:, start : start + BLK]
+        high = block.astype(BF)
+        low = (block - high.astype(F32)).astype(BF)
+        parts.append(
+            jnp.dot(high, had, preferred_element_type=F32) + jnp.dot(low, had, preferred_element_type=F32)
+        )
+    return jnp.concatenate(parts, axis=1)
+
+
+def reduce_kernel(
+    tok, cot, wg, wu, wd, had,
+    X, GU, DH,
+    W, WD, s1s, s1r, s2s, s2r, T, z1s, z1r, z2s, z2r, RA, RX, RB, RC, RD, RE,
+    load_sem, gz, gx, gc, gs, s1_out, s1_in, s2_out, s2_in, z1_out, z1_in, z2_out, z2_in, rx_in, r_in, r_out,
+):
+    me = Place()
+    loads = [pltpu.make_async_copy(wd, WD, load_sem.at[0])]
+    for q in range(NQ):
+        loads.append(pltpu.make_async_copy(wg.at[:, pl.ds(256 * q, 256)], W.at[NQ + q], load_sem.at[1 + q]))
+        loads.append(pltpu.make_async_copy(wu.at[:, pl.ds(256 * q, 256)], W.at[2 * NQ + q], load_sem.at[1 + NQ + q]))
+    for load in loads:
+        load.start()
+    me.meet()
+
+    other = me.slot(1 - me.zl, me.x, me.core)
+
+    def gather_own(s, own):
+        X[s, me.t] = own[...]
+        send(X.at[s, me.t], X.at[s, me.t], gs.at[s], gz.at[s], me.to_zl()).start()
+        for k in (1, 2, 3):
+            send(X.at[s, me.t], X.at[s, me.t], gs.at[s], gx.at[s, 0, k - 1], me.to_x(k)).start()
+
+    def gather_zl(s):
+        send(X.at[s, other], X.at[s, other], gs.at[s], gz.at[s], me.to_zl()).wait_recv()
+        for k in (1, 2, 3):
+            send(X.at[s, other], X.at[s, other], gs.at[s], gx.at[s, 1, k - 1], me.to_x(k)).start()
+
+    def to_core(s, zl, x, n):
+        block = X.at[s, me.slot(zl, x, me.core)]
+        send(block, block, gs.at[s], gc.at[s, n], me.to_core()).start()
+
+    def gather_x(s):
+        to_core(s, me.zl, me.x, 0)
+        to_core(s, 1 - me.zl, me.x, 4)
+        for j, zl in ((0, me.zl), (1, 1 - me.zl)):
+            for k in (1, 2, 3):
+                came = me.at_x(-k)
+                block = X.at[s, me.slot(zl, came, me.core)]
+                send(block, block, gs.at[s], gx.at[s, j, k - 1], me.to_x(k)).wait_recv()
+                to_core(s, zl, came, 4 * j + k)
+
+    def gather_core(s):
+        for j, zl in ((0, me.zl), (1, 1 - me.zl)):
+            for k in range(4):
+                block = X.at[s, me.slot(zl, me.at_x(-k), 1 - me.core)]
+                send(block, block, gs.at[s], gc.at[s, 4 * j + k], me.to_core()).wait_recv()
+
+    gather_own(0, cot)
+    gather_own(1, tok)
+    loads[0].wait()
+    for q in range(NQ):
+        W[q] = WD[pl.ds(256 * q, 256), :].T
+    gather_zl(0)
+    gather_zl(1)
+    gather_x(0)
+    gather_core(0)
+    for load in loads[1:]:
+        load.wait()
+
+    def partial(p, chunk):
+        s = jnp.where(p < NQ, 0, 1)
+        rows = X[s, pl.ds(4 * chunk, 4)].reshape(192, 512)
+        return jnp.dot(rows, W[p], preferred_element_type=F32)
+
+    def s1(p, way):
+        return send(s1s.at[p, way], s1r.at[p, way], s1_out, s1_in.at[p, way], me.dp_y(1 - 2 * way))
+
+    def s2(p, way):
+        return send(s2s.at[p, way], s2r.at[p, way], s2_out, s2_in.at[p, way], me.dp_y(1 - 2 * way))
+
+    def z1(p, way):
+        return send(z1s.at[p, way], z1r.at[p, way], z1_out, z1_in.at[p, way], me.dp_z(1 - 2 * way))
+
+    def z2(p, way):
+        return send(z2s.at[p, way], z2r.at[p, way], z2_out, z2_in.at[p, way], me.dp_z(1 - 2 * way))
+
+    def stage_a(p):
+        far = partial(p, me.at_y(2)).astype(BF)
+        for way in (0, 1):
+            s1s[p, way] = far[:, 128 * way : 128 * way + 128]
+            s1(p, way).start()
+
+    def stage_b(p):
+        for way in (0, 1):
+            near = partial(p, me.at_y(1 - 2 * way))
+            s1(p, way).wait_recv()
+            for half in (0, 1):
+                value = near[:, 128 * half : 128 * half + 128]
+                if half == way:
+                    value = value + s1r[p, way].astype(F32)
+                s2s[p, way, half] = value.astype(BF)
+            s2(p, way).start()
+
+    def stage_c(p):
+        own = partial(p, me.y)
+        s2(p, 0).wait_recv()
+        s2(p, 1).wait_recv()
+        for half in (0, 1):
+            value = own[:, 128 * half : 128 * half + 128]
+            value = value + s2r[p, 0, half].astype(F32) + s2r[p, 1, half].astype(F32)
+            T[p, half] = value.reshape(4, 48, 128)
+        for way in (0, 1):
+            z1s[p, way] = T[p, way, me.at_z(2)].astype(BF)
+            z1(p, way).start()
+
+    def stage_d(p):
+        for way in (0, 1):
+            z1(p, way).wait_recv()
+            for half in (0, 1):
+                value = T[p, half, me.at_z(1 - 2 * way)]
+                if half == way:
+                    value = value + z1r[p, way].astype(F32)
+                z2s[p, way, half] = value.astype(BF)
+            z2(p, way).start()
+
+    def stage_e(p):
+        z2(p, 0).wait_recv()
+        z2(p, 1).wait_recv()
+        halves = [
+            T[p, half, me.zh] + z2r[p, 0, half].astype(F32) + z2r[p, 1, half].astype(F32) for half in (0, 1)
+        ]
+        total = jnp.concatenate(halves, axis=1)
+
+        @pl.when(p < NQ)
+        def _():
+            RA[p] = inner_hadamard(total, had[...])
+
+        @pl.when(p >= NQ)
+        def _():
+            GU[p - NQ] = total
+
+    def rx(k):
+        return send(RA, RX.at[k - 1], r_out.at[k - 1], rx_in.at[k - 1], me.to_x(k))
+
+    rc = send(RB, RC, r_out.at[3], r_in.at[0], me.to_core())
+    rz = send(RD, RE, r_out.at[4], r_in.at[1], me.to_zl())
+
+    def rotate_0():
+        for k in (1, 2, 3):
+            rx(k).start()
+
+    def rotate_1():
+        for k in (1, 2, 3):
+            rx(k).wait_recv()
+
+        @pl.loop(0, NQ)
+        def _(q):
+            total = x_sign(me, me.x) * RA[q]
+            for k in (1, 2, 3):
+                total = total + x_sign(me, me.at_x(-k)) * RX[k - 1, q]
+            RB[q] = total
+
+        rc.start()
+
+    def rotate_2():
+        rc.wait_recv()
+
+        @pl.loop(0, NQ)
+        def _(q):
+            RD[q] = RC[q] + sign_of(me.core) * RB[q]
+
+        rz.start()
+
+    def rotate_3():
+        rz.wait_recv()
+
+        @pl.loop(0, NQ)
+        def _(q):
+            DH[q] = (RE[q] + sign_of(me.zl) * RD[q]) * (1.0 / math.sqrt(BLK * 16))
+
+    @pl.loop(0, NP + LAG_E)
+    def _(i):
+        @pl.when(i == 1)
+        def _():
+            gather_x(1)
+
+        @pl.when(i == 3)
+        def _():
+            gather_core(1)
+
+        @pl.when(i == ROT_0)
+        def _():
+            rotate_0()
+
+        @pl.when(i == ROT_0 + 6)
+        def _():
+            rotate_1()
+
+        @pl.when(i == ROT_0 + 8)
+        def _():
+            rotate_2()
+
+        for stage, lag in ((stage_a, 0), (stage_b, LAG_B), (stage_c, LAG_C), (stage_d, LAG_D), (stage_e, LAG_E)):
+
+            @pl.when((i >= lag) & (i < NP + lag))
+            def _(stage=stage, lag=lag):
+                stage(i - lag)
+
+    rotate_3()
+    for s in (0, 1):
+        sent = X.at[s, pl.ds(0, 15)]
+        send(sent, sent, gs.at[s], gz.at[s], me.to_zl()).wait_send()
+    send(s1s, s1r, s1_out, s1_in.at[0, 0], me.dp_y(1)).wait_send()
+    send(s2s, s2r, s2_out, s2_in.at[0, 0], me.dp_y(1)).wait_send()
+    send(z1s, z1r, z1_out, z1_in.at[0, 0], me.dp_z(1)).wait_send()
+    send(z2s, z2r, z2_out, z2_in.at[0, 0], me.dp_z(1)).wait_send()
+    for k in (1, 2, 3):
+        rx(k).wait_send()
+    rc.wait_send()
+    rz.wait_send()
+
+
+def reduce_phase(tokens, cotangent, w_gate, w_up, w_down):
+    whole = pl.BlockSpec(memory_space=pltpu.VMEM)
+    any_space = pl.BlockSpec(memory_space=pl.ANY)
+    dma = pltpu.SemaphoreType.DMA
+    rot = pltpu.VMEM((NQ, 48, 256), F32)
+    return pl.pallas_call(
+        reduce_kernel,
+        out_shape=(
+            jax.ShapeDtypeStruct((2, 16, 48, 512), BF),
+            jax.ShapeDtypeStruct((2 * NQ, 48, 256), F32),
+            jax.ShapeDtypeStruct((NQ, 48, 256), F32),
+        ),
+        in_specs=[whole, whole, any_space, any_space, any_space, whole],
+        out_specs=(whole, whole, whole),
+        scratch_shapes=[
+            pltpu.VMEM((NP, 512, 256), BF),
+            pltpu.VMEM((1792, 512), BF),
+            pltpu.VMEM((NP, 2, 192, 128), BF),
+            pltpu.VMEM((NP, 2, 192, 128), BF),
+            pltpu.VMEM((NP, 2, 2, 192, 128), BF),
+            pltpu.VMEM((NP, 2, 2, 192, 128), BF),
+            pltpu.VMEM((NP, 2, 4, 48, 128), F32),
+            pltpu.VMEM((NP, 2, 48, 128), BF),
+            pltpu.VMEM((NP, 2, 48, 128), BF),
+            pltpu.VMEM((NP, 2, 2, 48, 128), BF),
+            pltpu.VMEM((NP, 2, 2, 48, 128), BF),
+            rot, pltpu.VMEM((3, NQ, 48, 256), F32), rot, rot, rot, rot,
+            dma((15,)), dma((2,)), dma((2, 2, 3)), dma((2, 8)), dma((2,)),
+            dma, dma((NP, 2)), dma, dma((NP, 2)), dma, dma((NP, 2)), dma, dma((NP, 2)),
+            dma((3,)), dma((2,)), dma((5,)),
+        ],
+        compiler_params=pltpu.CompilerParams(
+            collective_id=0, has_side_effects=True, vmem_limit_bytes=56 * 1024 * 1024
+        ),
+        name="reduce_phase",
+    )(tokens, cotangent, w_gate, w_up, w_down, sylvester(BLK, BF))
+
+
 def per_device(tokens, w_gate, w_up, w_down, cotangent):
-    all_tokens, all_cotangent = (
-        lax.all_gather(tokens, "tensor", axis=0, tiled=True),
-        lax.all_gather(cotangent, "tensor", axis=0, tiled=True),
-    )
-    width = w_gate.shape[1]
-    paired = jnp.concatenate((w_gate, w_up), axis=1)
-    block_rows = all_tokens
-    sums = lax.psum_scatter(
-        jnp.dot(block_rows, paired, preferred_element_type=jnp.float32),
-        "dp",
-        scatter_dimension=0,
-        tiled=True,
-    )
-    gate = sums[:, :width]
-    up = sums[:, width:]
+    X, GU, DH = reduce_phase(tokens, cotangent, w_gate, w_up, w_down)
+    all_cotangent, all_tokens = X[0].reshape(768, 512), X[1].reshape(768, 512)
+    gate = GU[:NQ].transpose(1, 0, 2).reshape(48, 1792)
+    up = GU[NQ:].transpose(1, 0, 2).reshape(48, 1792)
+    d_hidden = DH.transpose(1, 0, 2).reshape(48, 1792)
     sigma = jax.nn.sigmoid(gate)
     silu_gate = gate * sigma
     hidden = (silu_gate * up).astype(jnp.bfloat16)
@@ -67,16 +390,6 @@
         (((0,), (0,)), ((), ())),
         preferred_element_type=jnp.float32,
     ).astype(jnp.bfloat16)
-    block_rows = all_cotangent
-    d_rotated = lax.psum_scatter(
-        lax.dot_general(
-            block_rows, w_down, (((1,), (1,)), ((), ())), preferred_element_type=jnp.float32
-        ),
-        "dp",
-        scatter_dimension=0,
-        tiled=True,
-    )
-    d_hidden = rotate(d_rotated)
     d_gate_pre = (d_hidden * up * sigma * (1.0 + gate * (1.0 - sigma))).astype(jnp.bfloat16)
     d_up_pre = (d_hidden * silu_gate).astype(jnp.bfloat16)
     grads_gate, grads_up = (

time: 564 us -> 386 us (0.68)
  waiting for transfers between devices: 425 us -> 232 us
  Pallas kernels: 0 us -> 109 us
  blocking collectives: 44.4 us -> 0 us
  matrix products: 40.5 us -> 19.3 us
  local copies, waits for them, and re-layouts: 20.6 us -> 5.05 us
  starting transfers between devices: 11.3 us -> 1.8 us
    reduce_scatter x2 -> x0, waiting for transfers between devices: 161 us -> none  [the longest x1 101 us: per_device(): lax.psum_scatter(jnp.dot(block_rows, paired, preferred_element_type=jnp.f...]
    pallas_call x0 -> x1, Pallas kernels: none -> 109 us  [reduce_phase(): pl.pallas_call(reduce_kernel, out_shape=(jax.ShapeDtypeStruct((2, 16, 48,...]
    all_gather x2 -> x0, blocking collectives: 44.4 us -> none  [the longest x1 22.6 us: per_device(): lax.all_gather(cotangent, 'tensor', axis=0, tiled=True)]
    ppermute x8 -> x4, waiting for transfers between devices: 70.5 us -> 29.9 us  [swapped(): return lax.ppermute(value, axis, pairs)]
    unnamed x7 -> x8, local copies, waits for them, and re-layouts: 20.5 us -> 2.11 us
    dot_general x2 -> x0, matrix products: 13.5 us -> none  [the longest x1 9.37 us: per_device(): jnp.dot(block_rows, paired, preferred_element_type=jnp.float32)]
    all_gather x1, waiting for transfers between devices: 42.2 us -> 51.8 us  [per_device(): lax.all_gather(rotated, 'dp', axis=0, tiled=True)]
    ppermute x8 -> x4, starting transfers between devices: 10.9 us -> 1.46 us  [swapped(): return lax.ppermute(value, axis, pairs)]
  transfers between devices with their start and end apart: 14 -> 8, of which waited for: 14 -> 8; matrix products, arithmetic and copies ran while one was open for 11% -> 5% of each run, Pallas kernels for 0% -> 0%
where the time goes in v1:
time: 386 us
  waiting for transfers between devices  232 us (60%)
  Pallas kernels  109 us (28%)
  matrix products  19.3 us (5%)
  between operations  14 us (4%)
  local copies, waits for them, and re-layouts  5.05 us (1%)
  other arithmetic  4.21 us (1%)
    pallas_call x1, Pallas kernels, reduce_phase(): pl.pallas_call(reduce_kernel, out_shape=(jax.ShapeDtypeStruct((2, 16, 48,...  109 us
    all_gather x1, waiting for transfers between devices, per_device(): lax.all_gather(d_up_pre, 'dp', axis=0, tiled=True)  62.1 us
    reduce_scatter x1, waiting for transfers between devices, per_device(): lax.psum_scatter(first + second, 'tensor', scatter_dimension=0, tiled=True)  60.8 us
    all_gather x1, waiting for transfers between devices, per_device(): lax.all_gather(rotated, 'dp', axis=0, tiled=True)  51.8 us
    ppermute x4, waiting for transfers between devices, swapped(): return lax.ppermute(value, axis, pairs)  29.9 us
    all_gather x1, waiting for transfers between devices, per_device(): lax.all_gather(d_gate_pre, 'dp', axis=0, tiled=True)  27.1 us
  transfers between devices with their start and end apart: 8, of which 8 were waited for; matrix products, arithmetic and copies ran while one was open for 5% of the time, Pallas kernels for 0%

profile of v1, /device:TPU:8, one launch (start us, length us, event | category | flops | bytes accessed | tf_op | source)
XLA Modules:
  0.0 386.0 jit_solution(3249744647923117089)
XLA Ops:
  7.3 0.8 fusion.2.had
  8.1 109.3 %reduce_phase.1 = (bf16[2,16,48,512]{3,2,1,0:T(8,128)(2,1)}, f32[14,48,256]{2,1,0:T(8,128)}, f32[7,48,256]{2,1,0:T(8,128)}) custom-call(bf16[48,512]{1,0:T(8,128)(2,1)} %tok.1, bf16[48,512]{1,0:T(8,128)(2,1)} %cot.1, bf16[512,1792]{1,0:T(8,128)(2,1)} %wg.1, bf16[512,1792]{1,0:T(8,128)(2,1)} %wu.1, bf16[1792,512]{1,0:T(8,128)(2,1)} %wd.1, ...), custom_call_target="tpu_custom_call" | custom-call | tf_op jit(solution)/shard_map/reduce_phase/pallas_call | solution.py:343
  117.3 1.0 copy.16
  118.3 1.2 slice_bitcast_fusion.1
  119.6 0.9 multiply_convert_fusion.2
  120.6 0.7 all-gather.6.cloned.1.call-update
  122.7 1.6 collective-permute-done
  124.4 10.1 %collective-permute-done.1 = f32[48,1792]{1,0:T(8,128)S(1)} collective-permute-done((f32[48,1792]{1,0:T(8,128)S(1)}, f32[48,1792]{1,0:T(8,128)S(1)}, u32[]{:S(2)}, u32[]{:S(2)}) %collective-permute-start.1) | collective-permute-done | bytes 344096 | tf_op jit(solution)/shard_map/ppermute | solution.py:24
  134.6 1.2 collective-permute-start.2
  135.7 9.8 %collective-permute-done.2 = f32[48,1792]{1,0:T(8,128)S(1)} collective-permute-done((f32[48,1792]{1,0:T(8,128)S(1)}, f32[48,1792]{1,0:T(8,128)S(1)}, u32[]{:S(2)}, u32[]{:S(2)}) %collective-permute-start.2) | collective-permute-done | bytes 344096 | tf_op jit(solution)/shard_map/ppermute | solution.py:24
  145.7 8.4 %collective-permute-done.3 = f32[48,1792]{1,0:T(8,128)S(1)} collective-permute-done((f32[48,1792]{1,0:T(8,128)S(1)}, f32[48,1792]{1,0:T(8,128)S(1)}, u32[]{:S(2)}, u32[]{:S(2)}) %collective-permute-start.3) | collective-permute-done | bytes 344096 | tf_op jit(solution)/shard_map/ppermute | solution.py:24
  154.1 0.7 multiply_convert_fusion.1
  155.1 27.1 %all-gather.4.cloned.1.call-done = bf16[768,1792]{1,0:T(8,128)(2,1)} async-done(((bf16[48,1792]{1,0:T(8,128)(2,1)}), bf16[768,1792]{1,0:T(8,128)(2,1)}) %all-gather.4.cloned.1.call-update) | async-done | bytes 2752528 | tf_op jit(solution)/shard_map/all_gather | solution.py:396
  182.2 3.4 fusion.6
  185.6 62.1 %all-gather.6.cloned.1.call-done = bf16[768,1792]{1,0:T(8,128)(2,1)} async-done(((bf16[48,1792]{1,0:T(8,128)(2,1)}), bf16[768,1792]{1,0:T(8,128)(2,1)}) %all-gather.6.cloned.1.call-update) | async-done | bytes 2752528 | tf_op jit(solution)/shard_map/all_gather | solution.py:397
  247.7 5.1 %convolution_add_fusion = f32[768,512]{1,0:T(8,128)} fusion(f32[768,512]{1,0:T(8,128)S(1)} %fusion.6, bf16[768,1792]{1,0:T(8,128)(2,1)} %all-gather.6.cloned.1.call-done, bf16[512,1792]{1,0:T(8,128)(2,1)} %wu.1), kind=kOutput, calls=%fused_computation.3 | convolution fusion | flops 1409679360 | bytes 7733248 | tf_op jit(solution)/shard_map/dot_general | solution.py:408
  252.8 1.4 copy-done.3
  254.3 0.7 copy-done
  255.0 2.9 convolution_convert_fusion.2
  257.9 2.9 convolution_convert_fusion.1
  260.8 51.8 %all-gather.8.cloned.1.call-done = bf16[768,1792]{1,0:T(8,128)(2,1)} async-done(((bf16[48,1792]{1,0:T(8,128)(2,1)}), bf16[768,1792]{1,0:T(8,128)(2,1)}) %all-gather.8.cloned.1.call-update) | async-done | bytes 2752528 | tf_op jit(solution)/shard_map/all_gather | solution.py:388
  312.6 4.6 %convolution_convert_fusion = bf16[1792,512]{1,0:T(8,128)(2,1)} fusion(bf16[768,1792]{1,0:T(8,128)(2,1)} %all-gather.8.cloned.1.call-done, bf16[768,512]{1,0:T(8,128)(2,1)S(1)} %bitcast.40), kind=kOutput, calls=%fused_computation | convolution fusion | flops 1410203648 | bytes 5373952 | tf_op jit(solution)/shard_map/dot_general | solution.py:387
  317.2 60.8 %reduce-scatter.2.cloned.1.call-done = f32[48,512]{1,0:T(8,128)} async-done(((f32[768,512]{1,0:T(8,128)}), f32[48,512]{1,0:T(8,128)}) %reduce-scatter.2.cloned.1.call-update) | async-done | bytes 98320 | tf_op jit(solution)/shard_map/reduce_scatter | solution.py:409
  378.0 1.5 convert_element_type.81
  (33 shorter events, 2.1 us)
Async XLA Ops:
  7.2 175.0 %all-gather.4.cloned.1.call-start = ((), (), s32[]{:S(2)}) async-start(), calls=%async_computation.1 | async-start | bytes 2924544 | tf_op jit(solution)/shard_map/all_gather | solution.py:396
  120.6 127.1 %all-gather.6.cloned.1.call-start = ((), (), s32[]{:S(2)}) async-start(), calls=%async_computation.2 | async-start | bytes 2924544 | tf_op jit(solution)/shard_map/all_gather | solution.py:397
  121.3 191.2 %all-gather.8.cloned.1.call-start = ((), (), s32[]{:S(2)}) async-start(), calls=%async_computation.4 | async-start | bytes 2924544 | tf_op jit(solution)/shard_map/all_gather | solution.py:388
  122.5 1.7 collective-permute-start
  122.6 59.5 %copy-start.2 = (bf16[512,1792]{1,0:T(8,128)(2,1)S(1)}, bf16[512,1792]{1,0:T(8,128)(2,1)}, u32[]{:S(2)}) copy-start(bf16[512,1792]{1,0:T(8,128)(2,1)} %wg.1) | copy-start | bytes 5505028
  124.3 10.2 %collective-permute-start.1 = (f32[48,1792]{1,0:T(8,128)S(1)}, f32[48,1792]{1,0:T(8,128)S(1)}, u32[]{:S(2)}, u32[]{:S(2)}) collective-permute-start(f32[48,1792]{1,0:T(8,128)S(1)} %add_select_fusion.2), channel_id=1, source_target_pairs={{0,2},{1,3},{2,0},{3,1},{4,6},{5,7},{6,4},{7,5},{8,10},{9,11},{10,... | collective-permute-start | bytes 1032200 | tf_op jit(solution)/shard_map/ppermute | solution.py:24
  134.6 11.0 %collective-permute-start.2 = (f32[48,1792]{1,0:T(8,128)S(1)}, f32[48,1792]{1,0:T(8,128)S(1)}, u32[]{:S(2)}, u32[]{:S(2)}) collective-permute-start(f32[48,1792]{1,0:T(8,128)S(1)} %add_select_fusion.1), channel_id=1, source_target_pairs={{0,4},{1,5},{2,6},{3,7},{4,0},{5,1},{6,2},{7,3},{8,12},{9,13},{10,... | collective-permute-start | bytes 1032200 | tf_op jit(solution)/shard_map/ppermute | solution.py:24
  145.6 8.5 %collective-permute-start.3 = (f32[48,1792]{1,0:T(8,128)S(1)}, f32[48,1792]{1,0:T(8,128)S(1)}, u32[]{:S(2)}, u32[]{:S(2)}) collective-permute-start(f32[48,1792]{1,0:T(8,128)S(1)} %add_select_fusion), channel_id=1, source_target_pairs={{0,8},{1,9},{2,10},{3,11},{4,12},{5,13},{6,14},{7,15},{8,0},{9,1},... | collective-permute-start | bytes 1032200 | tf_op jit(solution)/shard_map/ppermute | solution.py:24
  154.9 223.1 %reduce-scatter.2.cloned.1.call-start = ((), (), s32[]{:S(2)}) async-start(), calls=%async_computation.3 | async-start | bytes 1671168 | tf_op jit(solution)/shard_map/reduce_scatter | solution.py:409
  252.7 1.4 copy-start.3
  252.8 2.2 copy-start
  255.0 2.9 copy-start.1
Sparse Core Ops, SparseCore 0:
  120.7 61.4 all-gather.3
  185.2 62.3 all-gather.5
  250.1 62.3 all-gather.7
  315.0 62.9 reduce-scatter.1

commit v2 on v1

--- a/solution.py
+++ b/solution.py
@@ -16,12 +16,6 @@
 NP = 3 * NQ
 LAG_B, LAG_C, LAG_D, LAG_E = 1, 3, 4, 5
 ROT_0 = NQ + LAG_E
-
-
-def swapped(value, axis, distance):
-    mask = 2**distance
-    pairs = [(source, source ^ mask) for source in range(lax.axis_size(axis))]
-    return lax.ppermute(value, axis, pairs)
 
 
 def sylvester(order, dtype=jnp.float32):
@@ -33,21 +27,6 @@
         both = (row_ids >> power & 1) * (col_ids >> power & 1)
         signs = signs * (1 - 2 * both).astype(jnp.float32)
     return signs.astype(dtype)
-
-
-def rotate(values):
-    row_count, width = values.shape
-    shaped = values.reshape(row_count, width // BLK, BLK)
-    inner = jnp.einsum("mbj,jk->mbk", shaped, sylvester(BLK), precision=lax.Precision.HIGHEST)
-    inner = inner.reshape(row_count, width)
-    members = lax.axis_size("tensor")
-    position = lax.axis_index("tensor")
-    mixed = inner
-    for power in range(members.bit_length() - 1):
-        partner = swapped(mixed, "tensor", power)
-        upper = position >> power & 1 == 1
-        mixed = jnp.where(upper, partner - mixed, mixed + partner)
-    return mixed * (1.0 / math.sqrt(BLK * members))
 
 
 class Place:
@@ -373,42 +352,228 @@
     )(tokens, cotangent, w_gate, w_up, w_down, sylvester(BLK, BF))
 
 
+def spread_kernel(
+    gu, dh, wg, wu, had,
+    Gg, Gu, Gr, DT,
+    WG, WU, HID, HX, RB, RC, RD, RE, PT, PR, XR, SZ, ZR,
+    load_sem, out, zf, zhf, yf, yhf, hx_in, r_in, r_out, core_in, x_in, zl_in, t_out, x_out,
+):
+    me = Place()
+    loads = [pltpu.make_async_copy(wg, WG, load_sem.at[0]), pltpu.make_async_copy(wu, WU, load_sem.at[1])]
+    for load in loads:
+        load.start()
+    me.meet()
+    grads = (Gg, Gu, Gr)
+
+    def block(y, z):
+        return y * 4 + z
+
+    def part(s, index, half=None):
+        if half is None:
+            return grads[s].at[index]
+        return grads[s].at[index, :, pl.ds(896 * half, 896)]
+
+    def z_full(s, way, index):
+        return send(part(s, index), part(s, index), out.at[s], zf.at[s, way], me.dp_z(1 - 2 * way))
+
+    def z_half(s, way, index):
+        ref = part(s, index, way)
+        return send(ref, ref, out.at[s], zhf.at[s, way], me.dp_z(1 - 2 * way))
+
+    def y_full(s, way, r, index):
+        return send(part(s, index), part(s, index), out.at[s], yf.at[s, way, r], me.dp_y(1 - 2 * way))
+
+    def y_half(s, way, r, index):
+        ref = part(s, index, way)
+        return send(ref, ref, out.at[s], yhf.at[s, way, r], me.dp_y(1 - 2 * way))
+
+    def along_y(s, r):
+        for way in (0, 1):
+            y_full(s, way, r, block(me.y, me.at_z(r))).start()
+
+    def own_out(s):
+        for way in (0, 1):
+            z_full(s, way, me.dp).start()
+        along_y(s, 0)
+
+    def z_came(s):
+        for way, r in ((0, -1), (1, 1)):
+            index = block(me.y, me.at_z(r))
+            z_full(s, way, index).wait_recv()
+            z_half(s, way, index).start()
+            along_y(s, r % 4)
+
+    def z_done(s):
+        for way in (0, 1):
+            z_half(s, way, block(me.y, me.at_z(2))).wait_recv()
+        along_y(s, 2)
+
+    def y_came(s, r):
+        for way in (0, 1):
+            index = block(me.at_y(2 * way - 1), me.at_z(r))
+            y_full(s, way, r, index).wait_recv()
+            y_half(s, way, r, index).start()
+
+    def y_done(s, r):
+        for way in (0, 1):
+            y_half(s, way, r, block(me.at_y(2), me.at_z(r))).wait_recv()
+
+    def columns(q):
+        return slice(256 * q, 256 * q + 256)
+
+    for q in range(NQ):
+        gate, up, d_hidden = gu[q], gu[NQ + q], dh[q]
+        sigma = jax.nn.sigmoid(gate)
+        Gg[me.dp, :, columns(q)] = (d_hidden * up * sigma * (1.0 + gate * (1.0 - sigma))).astype(BF)
+    own_out(0)
+    for q in range(NQ):
+        gate, up, d_hidden = gu[q], gu[NQ + q], dh[q]
+        silu_gate = gate * jax.nn.sigmoid(gate)
+        HID[:, columns(q)] = (silu_gate * up).astype(BF)
+        Gu[me.dp, :, columns(q)] = (d_hidden * silu_gate).astype(BF)
+
+    def hx(k):
+        return send(HID, HX.at[k - 1], r_out.at[k - 1], hx_in.at[k - 1], me.to_x(k))
+
+    rc = send(RB, RC, r_out.at[3], r_in.at[0], me.to_core())
+    rz = send(RD, RE, r_out.at[4], r_in.at[1], me.to_zl())
+    for k in (1, 2, 3):
+        hx(k).start()
+    own_out(1)
+    z_came(0)
+    for k in (1, 2, 3):
+        hx(k).wait_recv()
+    for q in range(NQ):
+        total = x_sign(me, me.x) * HID[:, columns(q)].astype(F32)
+        for k in (1, 2, 3):
+            total = total + x_sign(me, me.at_x(-k)) * HX[k - 1, :, columns(q)].astype(F32)
+        RB[q] = inner_hadamard(total, had[...])
+    rc.start()
+    z_came(1)
+    z_done(0)
+    rc.wait_recv()
+    for q in range(NQ):
+        RD[q] = RC[q] + sign_of(me.core) * RB[q]
+    rz.start()
+    y_came(0, 0)
+    z_done(1)
+    y_came(1, 0)
+    rz.wait_recv()
+    for q in range(NQ):
+        total = (RE[q] + sign_of(me.zl) * RD[q]) * (1.0 / math.sqrt(BLK * 16))
+        Gr[me.dp, :, columns(q)] = total.astype(BF)
+    own_out(2)
+    for r in (3, 1, 2):
+        y_came(0, r)
+    z_came(2)
+    y_came(1, 3)
+    z_done(2)
+    for r in (1, 2):
+        y_came(1, r)
+    for load in loads:
+        load.wait()
+    for s in (0, 1):
+        for r in (0, 3, 1, 2):
+            y_done(s, r)
+
+    weights = (((1,), (1,)), ((), ()))
+    to_core = send(PT.at[1 - me.core], PR, t_out.at[0], core_in, me.to_core())
+
+    def term(core, half):
+        rows = [
+            jnp.concatenate([G[2 * j + core] for j in range(4 * half, 4 * half + 4)], axis=0) for G in (Gg, Gu)
+        ]
+        total = lax.dot_general(rows[0], WG[...], weights, preferred_element_type=F32)
+        total = total + lax.dot_general(rows[1], WU[...], weights, preferred_element_type=F32)
+        PT[core, pl.ds(4 * half, 4)] = total.reshape(4, 48, 512)
+
+    for half in (0, 1):
+        term(1 - me.core, half)
+    to_core.start()
+    for half in (0, 1):
+        term(me.core, half)
+    y_came(2, 0)
+    to_core.wait_recv()
+    for j in range(8):
+        PR[j] = PR[j] + PT[me.core, j]
+
+    def x_term(k, zl):
+        return send(
+            PR.at[4 * zl + me.at_x(k)], XR.at[k - 1, zl], x_out.at[k - 1, zl], x_in.at[k - 1, zl], me.to_x(k)
+        )
+
+    for k in (1, 2, 3):
+        for zl in (0, 1):
+            x_term(k, zl).start()
+    y_came(2, 3)
+    for k in (1, 2, 3):
+        for zl in (0, 1):
+            x_term(k, zl).wait_recv()
+    for zl in (0, 1):
+        SZ[zl] = PR[4 * zl + me.x] + XR[0, zl] + XR[1, zl] + XR[2, zl]
+    to_zl = send(SZ.at[1 - me.zl], ZR, t_out.at[1], zl_in, me.to_zl())
+    to_zl.start()
+    y_came(2, 1)
+    to_zl.wait_recv()
+    DT[...] = (SZ[me.zl] + ZR[...]).astype(BF)
+    y_came(2, 2)
+    for r in (0, 3, 1, 2):
+        y_done(2, r)
+    for s in (0, 1, 2):
+        sent = grads[s].at[pl.ds(0, 15)]
+        send(sent, sent, out.at[s], zf.at[s, 0], me.dp_y(1)).wait_send()
+    for k in (1, 2, 3):
+        hx(k).wait_send()
+        for zl in (0, 1):
+            x_term(k, zl).wait_send()
+    for copy in (rc, rz, to_core, to_zl):
+        copy.wait_send()
+
+
+def spread_phase(GU, DH, w_gate, w_up):
+    whole = pl.BlockSpec(memory_space=pltpu.VMEM)
+    any_space = pl.BlockSpec(memory_space=pl.ANY)
+    dma = pltpu.SemaphoreType.DMA
+    rot = pltpu.VMEM((NQ, 48, 256), F32)
+    full = jax.ShapeDtypeStruct((16, 48, 1792), BF)
+    return pl.pallas_call(
+        spread_kernel,
+        out_shape=(full, full, full, jax.ShapeDtypeStruct((48, 512), BF)),
+        in_specs=[whole, whole, any_space, any_space, whole],
+        out_specs=(whole,) * 4,
+        scratch_shapes=[
+            pltpu.VMEM((512, 1792), BF),
+            pltpu.VMEM((512, 1792), BF),
+            pltpu.VMEM((48, 1792), BF),
+            pltpu.VMEM((3, 48, 1792), BF),
+            rot, rot, rot, rot,
+            pltpu.VMEM((2, 8, 48, 512), F32),
+            pltpu.VMEM((8, 48, 512), F32),
+            pltpu.VMEM((3, 2, 48, 512), F32),
+            pltpu.VMEM((2, 48, 512), F32),
+            pltpu.VMEM((48, 512), F32),
+            dma((2,)), dma((3,)), dma((3, 2)), dma((3, 2)), dma((3, 2, 4)), dma((3, 2, 4)),
+            dma((3,)), dma((2,)), dma((5,)), dma, dma((3, 2)), dma, dma((2,)), dma((3, 2)),
+        ],
+        compiler_params=pltpu.CompilerParams(
+            collective_id=1, has_side_effects=True, vmem_limit_bytes=56 * 1024 * 1024
+        ),
+        name="spread_phase",
+    )(GU, DH, w_gate, w_up, sylvester(BLK, BF))
+
+
 def per_device(tokens, w_gate, w_up, w_down, cotangent):
     X, GU, DH = reduce_phase(tokens, cotangent, w_gate, w_up, w_down)
     all_cotangent, all_tokens = X[0].reshape(768, 512), X[1].reshape(768, 512)
-    gate = GU[:NQ].transpose(1, 0, 2).reshape(48, 1792)
-    up = GU[NQ:].transpose(1, 0, 2).reshape(48, 1792)
-    d_hidden = DH.transpose(1, 0, 2).reshape(48, 1792)
-    sigma = jax.nn.sigmoid(gate)
-    silu_gate = gate * sigma
-    hidden = (silu_gate * up).astype(jnp.bfloat16)
-    rotated = rotate(hidden.astype(jnp.float32)).astype(jnp.bfloat16)
-    block_rows = all_cotangent
-    d_down = lax.dot_general(
-        lax.all_gather(rotated, "dp", axis=0, tiled=True),
-        block_rows,
-        (((0,), (0,)), ((), ())),
-        preferred_element_type=jnp.float32,
-    ).astype(jnp.bfloat16)
-    d_gate_pre = (d_hidden * up * sigma * (1.0 + gate * (1.0 - sigma))).astype(jnp.bfloat16)
-    d_up_pre = (d_hidden * silu_gate).astype(jnp.bfloat16)
-    grads_gate, grads_up = (
-        lax.all_gather(d_gate_pre, "dp", axis=0, tiled=True),
-        lax.all_gather(d_up_pre, "dp", axis=0, tiled=True),
-    )
+    grads_gate, grads_up, rotated, d_tokens = spread_phase(GU, DH, w_gate, w_up)
     contract_rows = (((0,), (0,)), ((), ()))
-    d_gate = lax.dot_general(
-        all_tokens, grads_gate, contract_rows, preferred_element_type=jnp.float32
-    ).astype(jnp.bfloat16)
-    d_up = lax.dot_general(
-        all_tokens, grads_up, contract_rows, preferred_element_type=jnp.float32
-    ).astype(jnp.bfloat16)
-    contract_cols = (((1,), (1,)), ((), ()))
-    first = lax.dot_general(grads_gate, w_gate, contract_cols, preferred_element_type=jnp.float32)
-    second = lax.dot_general(grads_up, w_up, contract_cols, preferred_element_type=jnp.float32)
-    d_tokens = lax.psum_scatter(first + second, "tensor", scatter_dimension=0, tiled=True).astype(
-        jnp.bfloat16
-    )
+
+    def product(left, right):
+        return lax.dot_general(left, right, contract_rows, preferred_element_type=F32).astype(BF)
+
+    d_gate = product(all_tokens, grads_gate.reshape(768, 1792))
+    d_up = product(all_tokens, grads_up.reshape(768, 1792))
+    d_down = product(rotated.reshape(768, 1792), all_cotangent)
     return (d_tokens, d_gate, d_up, d_down)
 
 

time: 386 us -> 223 us (0.58)
  waiting for transfers between devices: 232 us -> 0 us
  Pallas kernels: 109 us -> 207 us
  between operations: 14 us -> 0.69 us
  matrix products: 19.3 us -> 10.5 us
    all_gather x3 -> x0, waiting for transfers between devices: 141 us -> none  [the longest x1 62.1 us: per_device(): lax.all_gather(d_up_pre, 'dp', axis=0, tiled=True)]
    pallas_call x0 -> x1, Pallas kernels: none -> 97.7 us  [spread_phase(): pl.pallas_call(spread_kernel, out_shape=(full, full, full, jax.ShapeDtype...]
    reduce_scatter x1 -> x0, waiting for transfers between devices: 60.8 us -> none  [per_device(): lax.psum_scatter(first + second, 'tensor', scatter_dimension=0, tiled=True)]
    ppermute x4 -> x0, waiting for transfers between devices: 29.9 us -> none  [swapped(): return lax.ppermute(value, axis, pairs)]
    dot_general x6 -> x3, matrix products: 19.3 us -> 10.5 us  [product(): lax.dot_general(left, right, contract_rows, preferred_element_type=F32)]
  transfers between devices with their start and end apart: 8 -> 0, of which waited for: 8 -> 0; matrix products, arithmetic and copies ran while one was open for 5% -> 0% of each run, Pallas kernels for 0% -> 0%
where the time goes in v2:
time: 223 us; the launch traced here: 221 us
  Pallas kernels  207 us (93%)
  matrix products  10.5 us (5%)
    pallas_call x1, Pallas kernels, reduce_phase(): pl.pallas_call(reduce_kernel, out_shape=(jax.ShapeDtypeStruct((2, 16, 48,...  109 us
    pallas_call x1, Pallas kernels, spread_phase(): pl.pallas_call(spread_kernel, out_shape=(full, full, full, jax.ShapeDtype...  97.7 us
    dot_general x3, matrix products, product(): lax.dot_general(left, right, contract_rows, preferred_element_type=F32)  10.5 us

profile of v2, /device:TPU:8, one launch (start us, length us, event | category | flops | bytes accessed | tf_op | source)
XLA Modules:
  0.0 220.9 jit_solution(561362233917841182)
XLA Ops:
  0.7 0.8 multiply_convert_fusion.had
  1.5 109.1 %reduce_phase.1 = (bf16[2,16,48,512]{3,2,1,0:T(8,128)(2,1)}, f32[14,48,256]{2,1,0:T(8,128)}, f32[7,48,256]{2,1,0:T(8,128)}) custom-call(bf16[48,512]{1,0:T(8,128)(2,1)} %tok.1, bf16[48,512]{1,0:T(8,128)(2,1)} %cot.1, bf16[512,1792]{1,0:T(8,128)(2,1)} %wg.3, bf16[512,1792]{1,0:T(8,128)(2,1)} %wu.3, bf16[1792,512]{1,0:T(8,128)(2,1)} %wd.1, ...), custom_call_target="tpu_custom_call" | custom-call | tf_op jit(solution)/shard_map/reduce_phase/pallas_call | solution.py:322
  110.5 1.5 fusion
  112.0 97.7 %spread_phase.1 = (bf16[16,48,1792]{2,1,0:T(8,128)(2,1)}, bf16[16,48,1792]{2,1,0:T(8,128)(2,1)}, bf16[16,48,1792]{2,1,0:T(8,128)(2,1)}, bf16[48,512]{1,0:T(8,128)(2,1)}) custom-call(f32[14,48,256]{2,1,0:T(8,128)} %get-tuple-element.11.gu, f32[7,48,256]{2,1,0:T(8,128)} %get-tuple-element.12.dh, bf16[512,1792]{1,0:T(8,128)(2,1)} %wg.3, bf16[512,1792]{1,0:T(8,128)(2,1)} %wu.3, ...), custom_call_target="tpu_custom_call" | custom-call | tf_op jit(solution)/shard_map/spread_phase/pallas_call | solution.py:539
  209.8 0.0 copy-start
  209.8 4.8 %convolution_convert_fusion.2 = bf16[512,1792]{1,0:T(8,128)(2,1)} fusion(bf16[768,512]{1,0:T(8,128)(2,1)S(1)} %bitcast.11, bf16[768,1792]{1,0:T(8,128)(2,1)} %bitcast.14), kind=kOutput, calls=%fused_computation.2 | convolution fusion | flops 1410203648 | bytes 5373952 | tf_op jit(solution)/shard_map/dot_general | solution.py:572
  214.5 0.0 copy-done
  214.5 0.0 copy-start.2
  214.5 2.9 %convolution_convert_fusion.1 = bf16[512,1792]{1,0:T(8,128)(2,1)} fusion(bf16[768,512]{1,0:T(8,128)(2,1)S(1)} %bitcast.12, bf16[768,1792]{1,0:T(8,128)(2,1)S(1)} %bitcast.13), kind=kOutput, calls=%fused_computation.1 | convolution fusion | flops 1410203648 | bytes 5373952 | tf_op jit(solution)/shard_map/dot_general | solution.py:572
  217.4 0.0 copy-done.2
  217.4 0.0 copy-start.1
  217.4 2.9 %convolution_convert_fusion = bf16[1792,512]{1,0:T(8,128)(2,1)} fusion(bf16[768,1792]{1,0:T(8,128)(2,1)S(1)} %bitcast.16, bf16[768,512]{1,0:T(8,128)(2,1)S(1)} %bitcast.15), kind=kOutput, calls=%fused_computation | convolution fusion | flops 1410203648 | bytes 5373952 | tf_op jit(solution)/shard_map/dot_general | solution.py:572
  220.3 0.0 copy-done.1
  220.3 0.6 copy.10
  (4 shorter events, 0.0 us)
Async XLA Ops:
  209.8 4.8 %copy-start = (bf16[16,48,1792]{2,1,0:T(8,128)(2,1)S(1)}, bf16[16,48,1792]{2,1,0:T(8,128)(2,1)}, u32[]{:S(2)}) copy-start(bf16[16,48,1792]{2,1,0:T(8,128)(2,1)} %get-tuple-element.16) | copy-start | bytes 8257540
  214.5 2.9 %copy-start.2 = (bf16[16,48,1792]{2,1,0:T(8,128)(2,1)S(1)}, bf16[16,48,1792]{2,1,0:T(8,128)(2,1)}, u32[]{:S(2)}) copy-start(bf16[16,48,1792]{2,1,0:T(8,128)(2,1)} %get-tuple-element.17) | copy-start | bytes 8257540
  217.4 2.9 %copy-start.1 = (bf16[48,512]{1,0:T(8,128)(2,1)S(1)}, bf16[48,512]{1,0:T(8,128)(2,1)}, u32[]{:S(2)}) copy-start(bf16[48,512]{1,0:T(8,128)(2,1)} %get-tuple-element.30) | copy-start | bytes 147460

commit v3 on v1

v3 whole, which is shorter than its diff:
```python
import functools
import math

import jax
import jax.numpy as jnp
from jax import lax
from jax.experimental import pallas as pl
from jax.experimental.pallas import tpu as pltpu
from jax.sharding import PartitionSpec as P

BLK = 128
BF = jnp.bfloat16
F32 = jnp.float32
MESH = pl.DeviceIdType.MESH
NQ = 7
NP = 3 * NQ
LAG_B, LAG_C, LAG_D, LAG_E = 1, 3, 4, 5
ROT_X, ROT_CORE, ROT_ZL, ROT_END = 12, 17, 18, 21
GRADS = 21
HID_X, HID_CORE, HID_ZL, HID_END = 27, 29, 30, 32
SPREAD = (0, 1, 2, 4, 6)
SUM_X, SUM_ZL = 34, 37
STEPS = HID_END + SPREAD[4] + NQ


def reduce_flag(p):
    return jnp.where(lax.rem(p, 4) == 3, 1, 0)


def grads_flag(q):
    return jnp.where(lax.rem(q, 3) == 2, 1, 0)


def rotated_flag(q):
    return jnp.where(q == 3, 1, 0)


def sylvester(order, dtype=jnp.float32):
    positions = jnp.arange(order, dtype=jnp.int32)
    row_ids = positions[:, None]
    col_ids = positions[None, :]
    signs = jnp.ones((order, order), jnp.float32)
    for power in range(order.bit_length() - 1):
        both = (row_ids >> power & 1) * (col_ids >> power & 1)
        signs = signs * (1 - 2 * both).astype(jnp.float32)
    return signs.astype(dtype)


def around(position, step):
    return lax.rem(position + step + 4, 4)


class Place:
    def __init__(self):
        self.dp = lax.axis_index("dp")
        self.t = lax.axis_index("tensor")
        self.y, self.zh = lax.div(self.dp, 4), lax.rem(self.dp, 4)
        self.zl = lax.div(self.t, 8)
        self.x = lax.rem(lax.div(self.t, 2), 4)
        self.core = lax.rem(self.t, 2)

    def axes(self, flag):
        return self.y + flag * (self.zh - self.y), self.zh + flag * (self.y - self.zh)

    def dp_of(self, flag, first, second):
        return {"dp": (4 - 3 * flag) * first + (1 + 3 * flag) * second, "tensor": self.t}

    def at_x(self, step):
        return lax.rem(self.x + step + 4, 4)

    def slot(self, zl, x, core):
        return zl * 8 + x * 2 + core

    def to_x(self, step):
        return {"dp": self.dp, "tensor": self.slot(self.zl, self.at_x(step), self.core)}

    def to_core(self):
        return {"dp": self.dp, "tensor": self.slot(self.zl, self.x, 1 - self.core)}

    def to_zl(self):
        return {"dp": self.dp, "tensor": self.slot(1 - self.zl, self.x, self.core)}

    def meet(self):
        peers = []
        for step in (1, -1):
            peers.append(self.dp_of(0, around(self.y, step), self.zh))
            peers.append(self.dp_of(0, self.y, around(self.zh, step)))
        peers += [self.to_x(k) for k in (1, 2, 3)] + [self.to_core(), self.to_zl()]
        barrier = pltpu.get_barrier_semaphore()
        for peer in peers:
            pl.semaphore_signal(barrier, inc=1, device_id=peer, device_id_type=MESH)
        pl.semaphore_wait(barrier, len(peers))


def send(src, dst, send_sem, recv_sem, to):
    return pltpu.make_async_remote_copy(
        src_ref=src, dst_ref=dst, send_sem=send_sem, recv_sem=recv_sem, device_id=to, device_id_type=MESH
    )


def sign_of(bit):
    return (1 - 2 * bit).astype(F32)


def x_sign(place, other):
    both = lax.rem(place.x, 2) * lax.rem(other, 2) + lax.div(place.x, 2) * lax.div(other, 2)
    return sign_of(lax.rem(both, 2))


def inner_hadamard(value, had):
    parts = []
    for start in range(0, value.shape[1], BLK):
        block = value[:, start : start + BLK]
        high = block.astype(BF)
        low = (block - high.astype(F32)).astype(BF)
        parts.append(
            jnp.dot(high, had, preferred_element_type=F32) + jnp.dot(low, had, preferred_element_type=F32)
        )
    return jnp.concatenate(parts, axis=1)


def layer_kernel(
    tok, cot, wg, wu, wd, had,
    DG, DU, DD, DT,
    X, XT, W, WD, s1s, s1r, s2s, s2r, T, z1s, z1r, z2s, z2r, GU, DH,
    RA, RX, RB, RC, RD, RE, HID, HX, HB, HC, HD, HE, AG, AR, OW, OD, PT, PR, XR, SZ, ZR,
    load_sem, gz, gx, gc, gs, s1_out, s1_in, s2_out, s2_in, z1_out, z1_in, z2_out, z2_in,
    rx_in, r_in, r_out, hx_in, h_in, h_out, ag_out, a2f, a2h, a1f, a1h, core_in, x_in, zl_in, t_out, x_out, o_sem,
):
    me = Place()
    loads = [pltpu.make_async_copy(wd, WD, load_sem.at[0])]
    for q in range(NQ):
        loads.append(pltpu.make_async_copy(wg.at[:, pl.ds(256 * q, 256)], W.at[NQ + 2 * q], load_sem.at[1 + q]))
        loads.append(pltpu.make_async_copy(wu.at[:, pl.ds(256 * q, 256)], W.at[NQ + 2 * q + 1], load_sem.at[1 + NQ + q]))
    for load in loads:
        load.start()
    me.meet()

    other = me.slot(1 - me.zl, me.x, me.core)

    def gather_own(s, own):
        X[s, me.t] = own[...]
        send(X.at[s, me.t], X.at[s, me.t], gs.at[s], gz.at[s], me.to_zl()).start()
        for k in (1, 2, 3):
            send(X.at[s, me.t], X.at[s, me.t], gs.at[s], gx.at[s, 0, k - 1], me.to_x(k)).start()

    def gather_zl(s):
        send(X.at[s, other], X.at[s, other], gs.at[s], gz.at[s], me.to_zl()).wait_recv()
        for k in (1, 2, 3):
            send(X.at[s, other], X.at[s, other], gs.at[s], gx.at[s, 1, k - 1], me.to_x(k)).start()

    def to_core(s, zl, x, n):
        block = X.at[s, me.slot(zl, x, me.core)]
        send(block, block, gs.at[s], gc.at[s, n], me.to_core()).start()

    def gather_x(s):
        to_core(s, me.zl, me.x, 0)
        to_core(s, 1 - me.zl, me.x, 4)
        for j, zl in ((0, me.zl), (1, 1 - me.zl)):
            for k in (1, 2, 3):
                came = me.at_x(-k)
                block = X.at[s, me.slot(zl, came, me.core)]
                send(block, block, gs.at[s], gx.at[s, j, k - 1], me.to_x(k)).wait_recv()
                to_core(s, zl, came, 4 * j + k)

    def gather_core(s):
        for j, zl in ((0, me.zl), (1, 1 - me.zl)):
            for k in range(4):
                block = X.at[s, me.slot(zl, me.at_x(-k), 1 - me.core)]
                send(block, block, gs.at[s], gc.at[s, 4 * j + k], me.to_core()).wait_recv()

    gather_own(0, cot)
    loads[0].wait()
    for q in range(3):
        W[q] = WD[pl.ds(256 * q, 256), :].T
    gather_zl(0)
    gather_own(1, tok)
    for q in range(3, NQ):
        W[q] = WD[pl.ds(256 * q, 256), :].T
    gather_zl(1)
    PT[...] = jnp.zeros_like(PT)
    gather_x(0)
    gather_core(0)
    for load in loads[1:]:
        load.wait()

    def partial(p, flag, first):
        s = jnp.where(p < NQ, 0, 1)
        rows = [X[s, (4 - 3 * flag) * first + (1 + 3 * flag) * j] for j in range(4)]
        return jnp.dot(jnp.concatenate(rows, axis=0), W[p], preferred_element_type=F32)

    def ring_1(p, way, src, dst, out, came):
        flag = reduce_flag(p)
        first, second = me.axes(flag)
        to = me.dp_of(flag, around(first, 1 - 2 * way), second)
        return send(src.at[p, way], dst.at[p, way], out, came.at[p, way], to)

    def ring_2(p, way, src, dst, out, came):
        flag = reduce_flag(p)
        first, second = me.axes(flag)
        to = me.dp_of(flag, first, around(second, 1 - 2 * way))
        return send(src.at[p, way], dst.at[p, way], out, came.at[p, way], to)

    def s1(p, way):
        return ring_1(p, way, s1s, s1r, s1_out, s1_in)

    def s2(p, way):
        return ring_1(p, way, s2s, s2r, s2_out, s2_in)

    def z1(p, way):
        return ring_2(p, way, z1s, z1r, z1_out, z1_in)

    def z2(p, way):
        return ring_2(p, way, z2s, z2r, z2_out, z2_in)

    def stage_a(p):
        flag = reduce_flag(p)
        far = partial(p, flag, around(me.axes(flag)[0], 2)).astype(BF)
        for way in (0, 1):
            s1s[p, way] = far[:, 128 * way : 128 * way + 128]
            s1(p, way).start()

    def stage_b(p):
        flag = reduce_flag(p)
        for way in (0, 1):
            near = partial(p, flag, around(me.axes(flag)[0], 1 - 2 * way))
            s1(p, way).wait_recv()
            for half in (0, 1):
                value = near[:, 128 * half : 128 * half + 128]
                if half == way:
                    value = value + s1r[p, way].astype(F32)
                s2s[p, way, half] = value.astype(BF)
            s2(p, way).start()

    def stage_c(p):
        flag = reduce_flag(p)
        first, second = me.axes(flag)
        own = partial(p, flag, first)
        s2(p, 0).wait_recv()
        s2(p, 1).wait_recv()
        for half in (0, 1):
            value = own[:, 128 * half : 128 * half + 128]
            value = value + s2r[p, 0, half].astype(F32) + s2r[p, 1, half].astype(F32)
            T[p, half] = value.reshape(4, 48, 128)
        for way in (0, 1):
            z1s[p, way] = T[p, way, around(second, 2)].astype(BF)
            z1(p, way).start()

    def stage_d(p):
        second = me.axes(reduce_flag(p))[1]
        for way in (0, 1):
            z1(p, way).wait_recv()
            for half in (0, 1):
                value = T[p, half, around(second, 1 - 2 * way)]
                if half == way:
                    value = value + z1r[p, way].astype(F32)
                z2s[p, way, half] = value.astype(BF)
            z2(p, way).start()

    def stage_e(p):
        second = me.axes(reduce_flag(p))[1]
        z2(p, 0).wait_recv()
        z2(p, 1).wait_recv()
        halves = [
            T[p, half, second] + z2r[p, 0, half].astype(F32) + z2r[p, 1, half].astype(F32) for half in (0, 1)
        ]
        total = jnp.concatenate(halves, axis=1)

        @pl.when(p < NQ)
        def _():
            RA[p] = inner_hadamard(total, had[...])

        @pl.when(p >= NQ)
        def _():
            GU[p - NQ] = total

    def outer(own, came, half_1, came_1, half_2, came_2, x_sem, in_sem, out_sem):
        def x_copy(k):
            return send(own, came.at[k - 1], out_sem.at[k - 1], x_sem.at[k - 1], me.to_x(k))

        core_copy = send(half_1, came_1, out_sem.at[3], in_sem.at[0], me.to_core())
        zl_copy = send(half_2, came_2, out_sem.at[4], in_sem.at[1], me.to_zl())

        def start():
            for k in (1, 2, 3):
                x_copy(k).start()

        def along_x(inner):
            for k in (1, 2, 3):
                x_copy(k).wait_recv()

            @pl.loop(0, NQ)
            def _(q):
                total = x_sign(me, me.x) * own[q].astype(F32)
                for k in (1, 2, 3):
                    total = total + x_sign(me, me.at_x(-k)) * came[k - 1, q].astype(F32)
                half_1[q] = inner(total)

            core_copy.start()

        def cores():
            core_copy.wait_recv()

            @pl.loop(0, NQ)
            def _(q):
                half_2[q] = came_1[q] + sign_of(me.core) * half_1[q]

            zl_copy.start()

        def along_zl(store):
            zl_copy.wait_recv()

            @pl.loop(0, NQ)
            def _(q):
                store(q, (came_2[q] + sign_of(me.zl) * half_2[q]) * (1.0 / math.sqrt(BLK * 16)))

        def finish():
            for k in (1, 2, 3):
                x_copy(k).wait_send()
            core_copy.wait_send()
            zl_copy.wait_send()

        return start, along_x, cores, along_zl, finish

    rot = outer(RA, RX, RB, RC, RD, RE, rx_in, r_in, r_out)
    hid = outer(HID, HX, HB, HC, HD, HE, hx_in, h_in, h_out)

    def gathering(buf, row, flag_of):
        def place(u):
            flag = flag_of(u)
            return flag, *me.axes(flag)

        def second_copy(u, way, at, half=None):
            flag, first, second = place(u)
            part = slice(None) if half is None else half
            ref = buf.at[u, part, 4 * first + at]
            sem = (a2f if half is None else a2h).at[row + u, way]
            return send(ref, ref, ag_out.at[row // NQ], sem, me.dp_of(flag, first, around(second, 1 - 2 * way)))

        def first_copy(u, way, at, half=None):
            flag, first, second = place(u)
            part = slice(None) if half is None else half
            ref = buf.at[u, part, pl.ds(4 * at, 4)]
            sem = (a1f if half is None else a1h).at[row + u, way]
            return send(ref, ref, ag_out.at[row // NQ], sem, me.dp_of(flag, around(first, 1 - 2 * way), second))

        def begin(u):
            for way in (0, 1):
                second_copy(u, way, place(u)[2]).start()

        def pass_second(u):
            for way in (0, 1):
                at = around(place(u)[2], 2 * way - 1)
                second_copy(u, way, at).wait_recv()
                second_copy(u, way, at, way).start()

        def begin_first(u):
            for way in (0, 1):
                second_copy(u, way, around(place(u)[2], 2), way).wait_recv()
            for way in (0, 1):
                first_copy(u, way, place(u)[1]).start()

        def pass_first(u):
            for way in (0, 1):
                at = around(place(u)[1], 2 * way - 1)
                first_copy(u, way, at).wait_recv()
                first_copy(u, way, at, way).start()

        def complete(u):
            for way in (0, 1):
                first_copy(u, way, around(place(u)[1], 2), way).wait_recv()

        def finish():
            sent = buf.at[:, :, pl.ds(0, 15)]
            send(sent, sent, ag_out.at[row // NQ], a2f.at[0, 0], me.to_zl()).wait_send()

        return begin, pass_second, begin_first, pass_first, complete, finish

    def own_position(flag):
        first, second = me.axes(flag)
        return 4 * first + second

    def in_order(flag, block):
        halves = []
        for half in (0, 1):
            rows = [block(half, (4 - 3 * flag) * (d // 4) + (1 + 3 * flag) * (d % 4)) for d in range(16)]
            halves.append(jnp.concatenate(rows, axis=0))
        return jnp.concatenate(halves, axis=1)

    grads = gathering(AG, 0, grads_flag)
    turned = gathering(AR, NQ, rotated_flag)

    def grads_begin(q):
        gate, up, d_hidden = GU[2 * q], GU[2 * q + 1], DH[q]
        sigma = jax.nn.sigmoid(gate)
        silu_gate = gate * sigma
        HID[q] = (silu_gate * up).astype(BF)
        pair = (
            (d_hidden * up * sigma * (1.0 + gate * (1.0 - sigma))).astype(BF),
            (d_hidden * silu_gate).astype(BF),
        )
        at = own_position(grads_flag(q))
        for s in (0, 1):
            for half in (0, 1):
                AG[q, half, at, s] = pair[s][:, 128 * half : 128 * half + 128]
        grads[0](q)

    def out_grad(q, s):
        to = (DG, DU)[s].at[:, pl.ds(pl.multiple_of(256 * q, 256), 256)]
        return pltpu.make_async_copy(OW.at[q, s], to, o_sem.at[q, s])

    def out_down(q):
        to = DD.at[pl.ds(pl.multiple_of(256 * q, 256), 256)]
        return pltpu.make_async_copy(OD.at[q], to, o_sem.at[q, 2])

    def grads_end(q):
        grads[4](q)
        flag = grads_flag(q)
        total = None
        for s in (0, 1):
            value = in_order(flag, lambda half, at: AG[q, half, at, s])
            OW[q, s] = jnp.dot(XT[...], value, preferred_element_type=F32).astype(BF)
            out_grad(q, s).start()
            term = lax.dot_general(
                value, W[NQ + 2 * q + s], (((1,), (1,)), ((), ())), preferred_element_type=F32
            )
            total = term if total is None else total + term
        for n in range(16):
            PT[n % 2, n // 2] += total[48 * n : 48 * n + 48]

    def rotated_store(q, value):
        at = own_position(rotated_flag(q))
        for half in (0, 1):
            AR[q, half, at] = value[:, 128 * half : 128 * half + 128].astype(BF)
        turned[0](q)

    def rotated_end(q):
        turned[4](q)
        value = in_order(rotated_flag(q), lambda half, at: AR[q, half, at])
        OD[q] = jnp.dot(value.T, X[0].reshape(768, 512), preferred_element_type=F32).astype(BF)
        out_down(q).start()

    sum_core = send(PT.at[1 - me.core], PR, t_out.at[0], core_in, me.to_core())
    sum_zl = send(SZ.at[1 - me.zl], ZR, t_out.at[1], zl_in, me.to_zl())

    def sum_x(k, zl):
        return send(
            PR.at[4 * zl + me.at_x(k)], XR.at[k - 1, zl], x_out.at[k - 1, zl], x_in.at[k - 1, zl], me.to_x(k)
        )

    def sum_1():
        sum_core.wait_recv()
        for j in range(8):
            PR[j] = PR[j] + PT[me.core, j]
        for k in (1, 2, 3):
            for zl in (0, 1):
                sum_x(k, zl).start()

    def sum_2():
        for k in (1, 2, 3):
            for zl in (0, 1):
                sum_x(k, zl).wait_recv()
        for zl in (0, 1):
            SZ[zl] = PR[4 * zl + me.x] + XR[0, zl] + XR[1, zl] + XR[2, zl]
        sum_zl.start()

    def store_d_hidden(q, value):
        DH[q] = value

    at_step = {
        1: lambda: gather_x(1),
        3: lambda: gather_core(1),
        ROT_X: rot[0],
        ROT_CORE: lambda: rot[1](lambda value: value),
        ROT_ZL: rot[2],
        ROT_END: lambda: rot[3](store_d_hidden),
        HID_CORE: lambda: hid[1](lambda value: inner_hadamard(value, had[...])),
        HID_ZL: hid[2],
        HID_END: lambda: hid[3](rotated_store),
        SUM_X: sum_1,
        SUM_ZL: sum_2,
    }
    stages = [(stage_a, 0, NP), (stage_b, LAG_B, NP), (stage_c, LAG_C, NP), (stage_d, LAG_D, NP), (stage_e, LAG_E, NP)]
    stages += [(grads_begin, GRADS, NQ)]
    stages += [(grads[n], GRADS + SPREAD[n], NQ) for n in (1, 2, 3)]
    stages += [(turned[n], HID_END + SPREAD[n], NQ) for n in (1, 2, 3)]
    stages += [(grads_end, GRADS + SPREAD[4], NQ), (rotated_end, HID_END + SPREAD[4], NQ)]

    @pl.loop(0, STEPS)
    def _(i):
        for step, work in at_step.items():
            pl.when(i == step)(work)
        for stage, first, count in stages:

            @pl.when((i >= first) & (i < first + count))
            def _(stage=stage, first=first):
                stage(i - first)

        @pl.when(i == 5)
        def _():
            XT[...] = X[1].reshape(768, 512).T

        pl.when(i == HID_X)(hid[0])
        pl.when(i == GRADS + SPREAD[4] + NQ - 1)(sum_core.start)

    sum_zl.wait_recv()
    DT[...] = (SZ[me.zl] + ZR[...]).astype(BF)
    for q in range(NQ):
        for s in (0, 1):
            out_grad(q, s).wait()
        out_down(q).wait()
    for s in (0, 1):
        sent = X.at[s, pl.ds(0, 15)]
        send(sent, sent, gs.at[s], gz.at[s], me.to_zl()).wait_send()
    for src, dst, out in ((s1s, s1r, s1_out), (s2s, s2r, s2_out), (z1s, z1r, z1_out), (z2s, z2r, z2_out)):
        send(src, dst, out, gz.at[0], me.to_zl()).wait_send()
    rot[4]()
    hid[4]()
    grads[5]()
    turned[5]()
    sum_core.wait_send()
    sum_zl.wait_send()
    for k in (1, 2, 3):
        for zl in (0, 1):
            sum_x(k, zl).wait_send()


def per_device(tokens, w_gate, w_up, w_down, cotangent):
    whole = pl.BlockSpec(memory_space=pltpu.VMEM)
    any_space = pl.BlockSpec(memory_space=pl.ANY)
    dma = pltpu.SemaphoreType.DMA
    part, part_bf = pltpu.VMEM((NQ, 48, 256), F32), pltpu.VMEM((NQ, 48, 256), BF)
    d_gate, d_up, d_down, d_tokens = pl.pallas_call(
        layer_kernel,
        out_shape=(
            jax.ShapeDtypeStruct((512, 1792), BF),
            jax.ShapeDtypeStruct((512, 1792), BF),
            jax.ShapeDtypeStruct((1792, 512), BF),
            jax.ShapeDtypeStruct((48, 512), BF),
        ),
        in_specs=[whole, whole, any_space, any_space, any_space, whole],
        out_specs=(any_space, any_space, any_space, whole),
        scratch_shapes=[
            pltpu.VMEM((2, 16, 48, 512), BF),
            pltpu.VMEM((512, 768), BF),
            pltpu.VMEM((NP, 512, 256), BF),
            pltpu.VMEM((1792, 512), BF),
            pltpu.VMEM((NP, 2, 192, 128), BF),
            pltpu.VMEM((NP, 2, 192, 128), BF),
            pltpu.VMEM((NP, 2, 2, 192, 128), BF),
            pltpu.VMEM((NP, 2, 2, 192, 128), BF),
            pltpu.VMEM((NP, 2, 4, 48, 128), F32),
            pltpu.VMEM((NP, 2, 48, 128), BF),
            pltpu.VMEM((NP, 2, 48, 128), BF),
            pltpu.VMEM((NP, 2, 2, 48, 128), BF),
            pltpu.VMEM((NP, 2, 2, 48, 128), BF),
            pltpu.VMEM((2 * NQ, 48, 256), F32),
            part,
            part, pltpu.VMEM((3, NQ, 48, 256), F32), part, part, part, part,
            part_bf, pltpu.VMEM((3, NQ, 48, 256), BF), part, part, part, part,
            pltpu.VMEM((NQ, 2, 16, 2, 48, 128), BF),
            pltpu.VMEM((NQ, 2, 16, 48, 128), BF),
            pltpu.VMEM((NQ, 2, 512, 256), BF),
            pltpu.VMEM((NQ, 256, 512), BF),
            pltpu.VMEM((2, 8, 48, 512), F32),
            pltpu.VMEM((8, 48, 512), F32),
            pltpu.VMEM((3, 2, 48, 512), F32),
            pltpu.VMEM((2, 48, 512), F32),
            pltpu.VMEM((48, 512), F32),
            dma((15,)), dma((2,)), dma((2, 2, 3)), dma((2, 8)), dma((2,)),
            dma, dma((NP, 2)), dma, dma((NP, 2)), dma, dma((NP, 2)), dma, dma((NP, 2)),
            dma((3,)), dma((2,)), dma((5,)), dma((3,)), dma((2,)), dma((5,)),
            dma((2,)), dma((2 * NQ, 2)), dma((2 * NQ, 2)), dma((2 * NQ, 2)), dma((2 * NQ, 2)),
            dma, dma((3, 2)), dma, dma((2,)), dma((3, 2)), dma((NQ, 3)),
        ],
        compiler_params=pltpu.CompilerParams(
            collective_id=0, has_side_effects=True, vmem_limit_bytes=60 * 1024 * 1024
        ),
        name="layer_backward",
    )(tokens, cotangent, w_gate, w_up, w_down, sylvester(BLK, BF))
    return (d_tokens, d_gate, d_up, d_down)


def solution(mesh):
    return jax.shard_map(
        per_device,
        mesh=mesh,
        in_specs=(
            P("tensor", "dp"),
            P("dp", "tensor"),
            P("dp", "tensor"),
            P("tensor", "dp"),
            P("tensor", "dp"),
        ),
        out_specs=(P("tensor", "dp"), P("dp", "tensor"), P("dp", "tensor"), P("tensor", "dp")),
        check_vma=False,
    )
```

time: 386 us -> 222 us (0.58)
  waiting for transfers between devices: 232 us -> 0 us
  Pallas kernels: 109 us -> 212 us
  matrix products: 19.3 us -> 0 us
  between operations: 14 us -> 0.67 us
    all_gather x3 -> x0, waiting for transfers between devices: 141 us -> none  [the longest x1 62.1 us: per_device(): lax.all_gather(d_up_pre, 'dp', axis=0, tiled=True)]
    pallas_call x1, Pallas kernels: 109 us -> 212 us  [per_device(): pl.pallas_call(layer_kernel, out_shape=(jax.ShapeDtypeStruct((512, 1792),...]
    reduce_scatter x1 -> x0, waiting for transfers between devices: 60.8 us -> none  [per_device(): lax.psum_scatter(first + second, 'tensor', scatter_dimension=0, tiled=True)]
    ppermute x4 -> x0, waiting for transfers between devices: 29.9 us -> none  [swapped(): return lax.ppermute(value, axis, pairs)]
    dot_general x6 -> x0, matrix products: 19.3 us -> none  [the longest x1 5.09 us: per_device(): lax.dot_general(grads_up, w_up, contract_cols, preferred_element_type=jnp...]
    unnamed x8, local copies, waits for them, and re-layouts: 2.11 us -> 7.79 us
  transfers between devices with their start and end apart: 8 -> 0, of which waited for: 8 -> 0; matrix products, arithmetic and copies ran while one was open for 5% -> 0% of each run, Pallas kernels for 0% -> 0%
where the time goes in v3:
time: 222 us
  Pallas kernels  212 us (95%)
  local copies, waits for them, and re-layouts  7.79 us (4%)
    pallas_call x1, Pallas kernels, per_device(): pl.pallas_call(layer_kernel, out_shape=(jax.ShapeDtypeStruct((512, 1792),...  212 us
    unnamed x8, local copies, waits for them, and re-layouts  7.79 us

profile of v3, /device:TPU:8, one launch (start us, length us, event | category | flops | bytes accessed | tf_op | source)
XLA Modules:
  0.0 221.7 jit_solution(5328719748288859898)
XLA Ops:
  0.7 0.8 multiply_convert_fusion.had
  1.5 212.4 %layer_backward.1 = (bf16[512,1792]{1,0:T(8,128)(2,1)}, bf16[512,1792]{1,0:T(8,128)(2,1)}, bf16[1792,512]{1,0:T(8,128)(2,1)}, bf16[48,512]{1,0:T(8,128)(2,1)}) custom-call(bf16[48,512]{1,0:T(8,128)(2,1)} %tok.1, bf16[48,512]{1,0:T(8,128)(2,1)} %cot.1, bf16[512,1792]{1,0:T(8,128)(2,1)} %wg.1, bf16[512,1792]{1,0:T(8,128)(2,1)} %wu.1, bf16[1792,512]{1,0:T(8,128)(2,1)} %wd.1, ...), custom_call_target="tpu_custom_call" | custom-call | tf_op jit(solution)/shard_map/layer_backward/pallas_call | solution.py:533
  213.9 1.4 copy.13
  215.3 0.0 copy-start.1
  215.3 3.0 %copy.14 = bf16[512,1792]{1,0:T(8,128)(2,1)} copy(bf16[512,1792]{1,0:T(8,128)(2,1)} %get-tuple-element.23) | data formatting | bytes 3670016
  218.3 0.0 copy-done.1
  218.3 0.0 copy-start
  218.3 1.2 copy.15
  219.5 0.9 copy-done
  220.5 1.2 copy.16
  (4 shorter events, 0.0 us)
Async XLA Ops:
  215.3 3.0 %copy-start.1 = (bf16[512,1792]{1,0:T(8,128)(2,1)S(1)}, bf16[512,1792]{1,0:T(8,128)(2,1)}, u32[]{:S(2)}) copy-start(bf16[512,1792]{1,0:T(8,128)(2,1)} %get-tuple-element.24) | copy-start | bytes 5505028
  218.3 2.2 copy-start

commit v4 on v3

--- a/solution.py
+++ b/solution.py
@@ -14,12 +14,12 @@
 MESH = pl.DeviceIdType.MESH
 NQ = 7
 NP = 3 * NQ
-LAG_B, LAG_C, LAG_D, LAG_E = 1, 3, 4, 5
-ROT_X, ROT_CORE, ROT_ZL, ROT_END = 12, 17, 18, 21
-GRADS = 21
-HID_X, HID_CORE, HID_ZL, HID_END = 27, 29, 30, 32
-SPREAD = (0, 1, 2, 4, 6)
-SUM_X, SUM_ZL = 34, 37
+LAG_B, LAG_C, LAG_D, LAG_E = 3, 6, 9, 12
+ROT_X, ROT_CORE, ROT_ZL, ROT_END = 19, 24, 26, 29
+GRADS = 29
+HID_X, HID_CORE, HID_ZL, HID_END = 35, 38, 41, 44
+SPREAD = (0, 4, 8, 14, 18)
+SUM_X, SUM_ZL = 54, 58
 STEPS = HID_END + SPREAD[4] + NQ
 
 
@@ -291,9 +291,9 @@
 
             @pl.loop(0, NQ)
             def _(q):
-                total = x_sign(me, me.x) * own[q].astype(F32)
+                total = x_sign(me, me.x) * own[q]
                 for k in (1, 2, 3):
-                    total = total + x_sign(me, me.at_x(-k)) * came[k - 1, q].astype(F32)
+                    total = total + x_sign(me, me.at_x(-k)) * came[k - 1, q]
                 half_1[q] = inner(total)
 
             core_copy.start()
@@ -344,21 +344,29 @@
             sem = (a1f if half is None else a1h).at[row + u, way]
             return send(ref, ref, ag_out.at[row // NQ], sem, me.dp_of(flag, around(first, 1 - 2 * way), second))
 
+        def along_first(u, at):
+            flag, first, second = place(u)
+            ref = buf.at[u, :, 4 * first + at]
+            for way in (0, 1):
+                to = me.dp_of(flag, around(first, 1 - 2 * way), second)
+                send(ref, ref, ag_out.at[row // NQ], a1f.at[row + u, way], to).start()
+
         def begin(u):
             for way in (0, 1):
                 second_copy(u, way, place(u)[2]).start()
+            along_first(u, place(u)[2])
 
         def pass_second(u):
             for way in (0, 1):
                 at = around(place(u)[2], 2 * way - 1)
                 second_copy(u, way, at).wait_recv()
                 second_copy(u, way, at, way).start()
+                along_first(u, at)
 
         def begin_first(u):
             for way in (0, 1):
                 second_copy(u, way, around(place(u)[2], 2), way).wait_recv()
-            for way in (0, 1):
-                first_copy(u, way, place(u)[1]).start()
+            along_first(u, around(place(u)[2], 2))
 
         def pass_first(u):
             for way in (0, 1):
@@ -394,7 +402,7 @@
         gate, up, d_hidden = GU[2 * q], GU[2 * q + 1], DH[q]
         sigma = jax.nn.sigmoid(gate)
         silu_gate = gate * sigma
-        HID[q] = (silu_gate * up).astype(BF)
+        HID[q] = silu_gate * up
         pair = (
             (d_hidden * up * sigma * (1.0 + gate * (1.0 - sigma))).astype(BF),
             (d_hidden * silu_gate).astype(BF),
@@ -529,7 +537,7 @@
     whole = pl.BlockSpec(memory_space=pltpu.VMEM)
     any_space = pl.BlockSpec(memory_space=pl.ANY)
     dma = pltpu.SemaphoreType.DMA
-    part, part_bf = pltpu.VMEM((NQ, 48, 256), F32), pltpu.VMEM((NQ, 48, 256), BF)
+    part = pltpu.VMEM((NQ, 48, 256), F32)
     d_gate, d_up, d_down, d_tokens = pl.pallas_call(
         layer_kernel,
         out_shape=(
@@ -557,7 +565,7 @@
             pltpu.VMEM((2 * NQ, 48, 256), F32),
             part,
             part, pltpu.VMEM((3, NQ, 48, 256), F32), part, part, part, part,
-            part_bf, pltpu.VMEM((3, NQ, 48, 256), BF), part, part, part, part,
+            part, pltpu.VMEM((3, NQ, 48, 256), F32), part, part, part, part,
             pltpu.VMEM((NQ, 2, 16, 2, 48, 128), BF),
             pltpu.VMEM((NQ, 2, 16, 48, 128), BF),
             pltpu.VMEM((NQ, 2, 512, 256), BF),

time: 222 us -> 198 us (0.89); the launches traced: 222 us -> 195 us
  Pallas kernels: 212 us -> 185 us
    pallas_call x1, Pallas kernels: 212 us -> 185 us  [per_device(): pl.pallas_call(layer_kernel, out_shape=(jax.ShapeDtypeStruct((512, 1792),...]
where the time goes in v4:
time: 198 us; the launch traced here: 195 us
  Pallas kernels  185 us (93%)
  local copies, waits for them, and re-layouts  7.79 us (4%)
    pallas_call x1, Pallas kernels, per_device(): pl.pallas_call(layer_kernel, out_shape=(jax.ShapeDtypeStruct((512, 1792),...  185 us
    unnamed x8, local copies, waits for them, and re-layouts  7.79 us

profile of v4, /device:TPU:8, one launch (start us, length us, event | category | flops | bytes accessed | tf_op | source)
XLA Modules:
  0.0 194.6 jit_solution(12413741728194245687)
XLA Ops:
  0.7 0.8 multiply_convert_fusion.had
  1.5 185.4 %layer_backward.1 = (bf16[512,1792]{1,0:T(8,128)(2,1)}, bf16[512,1792]{1,0:T(8,128)(2,1)}, bf16[1792,512]{1,0:T(8,128)(2,1)}, bf16[48,512]{1,0:T(8,128)(2,1)}) custom-call(bf16[48,512]{1,0:T(8,128)(2,1)} %tok.1, bf16[48,512]{1,0:T(8,128)(2,1)} %cot.1, bf16[512,1792]{1,0:T(8,128)(2,1)} %wg.1, bf16[512,1792]{1,0:T(8,128)(2,1)} %wu.1, bf16[1792,512]{1,0:T(8,128)(2,1)} %wd.1, ...), custom_call_target="tpu_custom_call" | custom-call | tf_op jit(solution)/shard_map/layer_backward/pallas_call | solution.py:541
  186.8 1.4 copy.13
  188.3 0.0 copy-start.1
  188.3 3.0 %copy.14 = bf16[512,1792]{1,0:T(8,128)(2,1)} copy(bf16[512,1792]{1,0:T(8,128)(2,1)} %get-tuple-element.23) | data formatting | bytes 3670016
  191.3 0.0 copy-done.1
  191.3 0.0 copy-start
  191.3 1.2 copy.15
  192.5 0.9 copy-done
  193.4 1.2 copy.16
  (4 shorter events, 0.0 us)
Async XLA Ops:
  188.3 3.0 %copy-start.1 = (bf16[512,1792]{1,0:T(8,128)(2,1)S(1)}, bf16[512,1792]{1,0:T(8,128)(2,1)}, u32[]{:S(2)}) copy-start(bf16[512,1792]{1,0:T(8,128)(2,1)} %get-tuple-element.24) | copy-start | bytes 5505028
  191.3 2.2 %copy-start = (bf16[1792,512]{1,0:T(8,128)(2,1)S(1)}, bf16[1792,512]{1,0:T(8,128)(2,1)}, u32[]{:S(2)}) copy-start(bf16[1792,512]{1,0:T(8,128)(2,1)} %get-tuple-element.25) | copy-start | bytes 5505028

commit v5 on v4

--- a/solution.py
+++ b/solution.py
@@ -28,7 +28,7 @@
 
 
 def grads_flag(q):
-    return jnp.where(lax.rem(q, 3) == 2, 1, 0)
+    return jnp.where(q == 3, 1, 0)
 
 
 def rotated_flag(q):

time: 198 us -> 197 us (level)
  no operation moved by 1% of the time
where the time goes in v5:
time: 197 us; the launch traced here: 195 us
  Pallas kernels  186 us (94%)
  local copies, waits for them, and re-layouts  7.79 us (4%)
    pallas_call x1, Pallas kernels, per_device(): pl.pallas_call(layer_kernel, out_shape=(jax.ShapeDtypeStruct((512, 1792),...  186 us
    unnamed x8, local copies, waits for them, and re-layouts  7.79 us

profile of v5, /device:TPU:8, one launch (start us, length us, event | category | flops | bytes accessed | tf_op | source)
XLA Modules:
  0.0 195.4 jit_solution(6636258744568080738)
XLA Ops:
  0.7 0.8 multiply_convert_fusion.had
  1.5 186.2 %layer_backward.1 = (bf16[512,1792]{1,0:T(8,128)(2,1)}, bf16[512,1792]{1,0:T(8,128)(2,1)}, bf16[1792,512]{1,0:T(8,128)(2,1)}, bf16[48,512]{1,0:T(8,128)(2,1)}) custom-call(bf16[48,512]{1,0:T(8,128)(2,1)} %tok.1, bf16[48,512]{1,0:T(8,128)(2,1)} %cot.1, bf16[512,1792]{1,0:T(8,128)(2,1)} %wg.1, bf16[512,1792]{1,0:T(8,128)(2,1)} %wu.1, bf16[1792,512]{1,0:T(8,128)(2,1)} %wd.1, ...), custom_call_target="tpu_custom_call" | custom-call | tf_op jit(solution)/shard_map/layer_backward/pallas_call | solution.py:541
  187.6 1.4 copy.13
  189.1 0.0 copy-start.1
  189.1 3.0 %copy.14 = bf16[512,1792]{1,0:T(8,128)(2,1)} copy(bf16[512,1792]{1,0:T(8,128)(2,1)} %get-tuple-element.23) | data formatting | bytes 3670016
  192.0 0.0 copy-done.1
  192.0 0.0 copy-start
  192.1 1.2 copy.15
  193.3 0.9 copy-done
  194.2 1.2 copy.16
  (4 shorter events, 0.0 us)
Async XLA Ops:
  189.1 3.0 %copy-start.1 = (bf16[512,1792]{1,0:T(8,128)(2,1)S(1)}, bf16[512,1792]{1,0:T(8,128)(2,1)}, u32[]{:S(2)}) copy-start(bf16[512,1792]{1,0:T(8,128)(2,1)} %get-tuple-element.24) | copy-start | bytes 5505028
  192.0 2.2 %copy-start = (bf16[1792,512]{1,0:T(8,128)(2,1)S(1)}, bf16[1792,512]{1,0:T(8,128)(2,1)}, u32[]{:S(2)}) copy-start(bf16[1792,512]{1,0:T(8,128)(2,1)} %get-tuple-element.25) | copy-start | bytes 5505028
